TPU v7x, 256 devices: a whole 4x4x8 slice. The times are simulated.
256 devices in a mesh: lat: 16 (over y, x), lon: 16 (over z, core).
Axes of the slice: x: 4, y: 4, z: 8, core: 2. Of those that a mesh axis runs over, the one named last changes fastest.
Arguments:
- innovation: float32 [64, 16384], P(None, ('lat', 'lon')), may hold values from -6 to 6
- obs_weight: float32 [64, 16384], P(None, ('lat', 'lon')), may hold values from 0.5 to 4
- jacobian: float32 [49152, 64, 128], P(('lat', 'lon')), may hold values from -0.5 to 0.5
- block_list: int32 [2, 49152], P(None, ('lat', 'lon')), may hold values from 0 to 1024, as said below
- pass_counts: int32 [2], replicated, may hold values from 3 to 6, as said below
- kappa_h: float32 [256, 512, 128], P('lat', 'lon'), may hold values from 0.03 to 0.24
- kappa_v: float32 [256, 512, 128], P('lat', 'lon'), may hold values from 0.05 to 0.45
Outputs:
- increment: float32 [256, 512, 128], P('lat', 'lon')
- residual: float32 [256, 512, 128], P('lat', 'lon')
Inputs may be any that keep to these rules, and one draw needn't show every extreme that they name: `pass_counts`: entry 0 counts lateral passes and entry 1 vertical passes; one of the two is 6 and the other is smaller. `block_list`: on each device the non-empty slots come first among its 192 slots, and in every latitude band some device has all 192 slots non-empty; an empty slot has block row 1024.
All inputs are finite; a program needn't handle non-finite values.
Results may differ from a plain program's by a relative error of at most 0.0003.
Values sent between devices are 32-bit elements; how exact they have to be, the bound alone decides.
A program may use at most 64 MiB of HBM per device.

v0:
```python
import jax
import jax.numpy as jnp
from jax import lax
from jax.sharding import PartitionSpec as P

ITERS = 2


def extended(block, sides, width):
    for axis, dim in sides:
        count = lax.axis_size(axis)
        forward = [(i, i + 1) for i in range(count - 1)]
        forward.append((count - 1, 0))
        backward = [(target, source) for source, target in forward]
        low = lax.ppermute(
            lax.slice_in_dim(block, block.shape[dim] - width, None, axis=dim), axis, forward
        )
        high = lax.ppermute(lax.slice_in_dim(block, 0, width, axis=dim), axis, backward)
        block = jnp.concatenate([low, block, high], axis=dim)
    return block


def vertical_faces(kappa_v):
    upper_face = jnp.sqrt(kappa_v[..., :-1] * kappa_v[..., 1:])
    zero_face = jnp.zeros(kappa_v.shape[:-1] + (1,), jnp.float32)
    return (
        jnp.concatenate([upper_face, zero_face], -1),
        jnp.concatenate([zero_face, upper_face], -1),
    )


def vertical_pass(current, face_below, face_above):
    zero_face = jnp.zeros(current.shape[:-1] + (1,), jnp.float32)
    higher = jnp.concatenate([current[..., 1:], zero_face], -1)
    lower_level = jnp.concatenate([zero_face, current[..., :-1]], -1)
    return current + face_below * (higher - current) + face_above * (lower_level - current)


def side_faces(padded):
    centre = padded[1:-1, 1:-1]
    return (
        jnp.sqrt(centre * padded[:-2, 1:-1]),
        jnp.sqrt(centre * padded[2:, 1:-1]),
        jnp.sqrt(centre * padded[1:-1, :-2]),
        jnp.sqrt(centre * padded[1:-1, 2:]),
    )


def side_pass(current, padded, face_set):
    return (
        current
        + face_set[0] * (padded[:-2, 1:-1] - current)
        + face_set[1] * (padded[2:, 1:-1] - current)
        + face_set[2] * (padded[1:-1, :-2] - current)
        + face_set[3] * (padded[1:-1, 2:] - current)
    )


def clear_poles(padded, margin):
    row_count = padded.shape[0]
    at_first = lax.axis_index("lat") == 0
    at_last = lax.axis_index("lat") == lax.axis_size("lat") - 1
    row_place = lax.broadcasted_iota(jnp.int32, padded.shape, 0)
    polar = at_first & (row_place < margin) | at_last & (row_place >= row_count - margin)
    return jnp.where(polar, 0.0, padded)


def local(innovation, obs_weight, jacobian, block_list, pass_counts, kappa_h, kappa_v):
    lat_cells, lon_cells, level_count = kappa_h.shape
    column_count = lat_cells * lon_cells
    own_rows = innovation.shape[1]
    band_rows = own_rows * lax.axis_size("lon")
    lateral_count = pass_counts[0]
    vertical_count = pass_counts[1]
    face_below, face_above = vertical_faces(kappa_v)
    highest = lax.Precision.HIGHEST
    kappa_pad = clear_poles(extended(kappa_h, (("lat", 0), ("lon", 1)), 1), 1)
    near_faces = side_faces(kappa_pad)

    def lateral(current):

        def single(counter, running):
            padded = extended(running, (("lat", 0), ("lon", 1)), 1)
            return side_pass(running, padded, near_faces)

        return lax.fori_loop(0, lateral_count, single, current)

    def vertical(current):
        return lax.fori_loop(
            0,
            vertical_count,
            lambda counter, running: vertical_pass(running, face_below, face_above),
            current,
        )

    def spread(current):
        return lateral(vertical(current))

    def spread_adjoint(current):
        return vertical(lateral(current))

    block_rows = block_list[0]
    block_cols = block_list[1]
    row_hot = (block_rows[:, None] == jnp.arange(band_rows, dtype=jnp.int32)[None, :]).astype(
        jnp.float32
    )
    col_hot = (block_cols[None, :] == jnp.arange(column_count, dtype=jnp.int32)[:, None]).astype(
        jnp.float32
    )
    weighted = obs_weight * innovation

    def observe_adjoint(band_weighted):
        taken = jnp.dot(band_weighted, row_hot.T, precision=highest)
        contrib = jnp.einsum("sok,os->sk", jacobian, taken, precision=highest)
        return jnp.dot(col_hot, contrib, precision=highest).reshape(
            lat_cells, lon_cells, level_count
        )

    band_weighted, band_weight = (
        lax.all_gather(weighted, "lon", axis=1, tiled=True),
        lax.all_gather(obs_weight, "lon", axis=1, tiled=True),
    )
    gradient = spread_adjoint(observe_adjoint(band_weighted))
    solution = jnp.zeros_like(gradient)
    residual = gradient
    direction = gradient
    norm_now = lax.psum(jnp.sum(residual * residual), ("lat", "lon"))
    for iteration in range(ITERS):
        picked = jnp.take(spread(direction).reshape(column_count, level_count), block_cols, axis=0)
        block_obs = jnp.einsum("sok,sk->os", jacobian, picked, precision=highest)
        all_obs = lax.psum(jnp.dot(block_obs, row_hot, precision=highest), "lon")
        band_back = band_weight * all_obs
        image_vec = direction + spread_adjoint(observe_adjoint(band_back))
        curvature_sum = lax.psum(jnp.sum(direction * image_vec), ("lat", "lon"))
        image_vec, curvature_sum = (image_vec, curvature_sum)
        alpha_step = norm_now / curvature_sum
        solution = solution + alpha_step * direction
        residual = residual - alpha_step * image_vec
        if iteration + 1 < ITERS:
            norm_next = lax.psum(jnp.sum(residual * residual), ("lat", "lon"))
            direction = residual + norm_next / norm_now * direction
            norm_now = norm_next
    return (spread(solution), residual)


def solution(mesh):
    return jax.shard_map(
        local,
        mesh=mesh,
        in_specs=(
            P(None, ("lat", "lon")),
            P(None, ("lat", "lon")),
            P(("lat", "lon"), None, None),
            P(None, ("lat", "lon")),
            P(),
            P("lat", "lon", None),
            P("lat", "lon", None),
        ),
        out_specs=(P("lat", "lon", None), P("lat", "lon", None)),
        check_vma=False,
    )
```

profile of v0, /device:TPU:9, one launch (start us, length us, event | category | flops | bytes accessed | tf_op | source)
XLA Modules:
  0.0 819.9 jit_solution(16119502304886370937)
XLA Ops:
  9.3 2.4 collective-permute-start.25
  14.1 22.5 %all_gather.6 = f32[64,1024]{0,1:T(8,128)S(1)} all-gather(f32[64,64]{0,1:T(8,128)S(1)} %mul.170), channel_id=1, replica_groups=mesh['lat'=16,'lon'=16] {'lon'}, dimensions={1}, use_global_device_ids=true | all-gather | bytes 278528 | tf_op jit(solution)/shard_map/all_gather | solution.py:120
  37.1 7.4 fusion.117
  47.1 1.9 collective-permute-done.27
  49.5 34.2 %while.120 = (s32[]{:T(128)}, f32[16,32,128]{2,1,0:T(8,128)S(1)}, s32[]{:T(128)}, f32[16,32,128]{2,1,0:T(8,128)S(1)}, f32[16,32,128]{2,1,0:T(8,128)S(1)}, /*inde...) while((s32[]{:T(128)}, f32[16,32,128]{2,1,0:T(8,128)S(1)}, s32[]{:T(128)}, ...), condition=%wide.region_1.2_spmd, body=%wide.region_0.1_spmd.sunk | while | flops 1048578 | bytes 3340533 | solution.py:86
  50.2 3.6 collective-permute-start.1
  55.0 2.5 collective-permute-start.2
  60.9 3.6 collective-permute-start.1
  65.7 4.8 collective-permute-start.2
  73.4 3.0 collective-permute-start.1
  77.6 4.1 collective-permute-start.2
  83.6 6.7 while.121
  90.3 6.7 while.122
  97.0 34.7 %while.123 = (s32[]{:T(128)}, f32[16,32,128]{2,1,0:T(8,128)S(1)}, s32[]{:T(128)}, f32[16,32,128]{2,1,0:T(8,128)S(1)}, f32[16,32,128]{2,1,0:T(8,128)S(1)}, /*inde...) while((s32[]{:T(128)}, f32[16,32,128]{2,1,0:T(8,128)S(1)}, s32[]{:T(128)}, ...), condition=%wide.region_9.10_spmd, body=%wide.region_8.9_spmd.sunk | while | flops 1048578 | bytes 3340533 | solution.py:86
  98.9 2.8 collective-permute-start.5
  102.8 4.0 collective-permute-start.6
  110.1 2.8 collective-permute-start.5
  114.0 4.0 collective-permute-start.6
  121.4 2.8 collective-permute-start.5
  125.3 4.0 collective-permute-start.6
  132.5 11.9 %fusion.118 = f32[192,1,64]{2,1,0:T(1,128)S(1)} fusion(f32[192,128,1]{1,2,0:T(1,128)S(1)} %bitcast.56, f32[192,64,128]{2,1,0:T(8,128)} %param.35), kind=kOutput, calls=%fused_computation.193 | convolution fusion | flops 18874368 | bytes 6438912 | tf_op jit(solution)/shard_map/sok,sk->os/dot_general | solution.py:130
  144.4 1.9 fusion.75
  146.4 18.7 %all_gather.7 = f32[64,1024]{0,1:T(8,128)S(1)} all-gather(f32[64,64]{0,1:T(8,128)S(1)} %copy.9), channel_id=1, replica_groups=mesh['lat'=16,'lon'=16] {'lon'}, dimensions={1}, use_global_device_ids=true | all-gather | bytes 278528 | tf_op jit(solution)/shard_map/all_gather | solution.py:121
  165.1 99.5 %all-reduce.18.cloned.1.call-done = f32[64,1024]{0,1:T(8,128)} async-done(((f32[64,1024]{0,1:T(8,128)}), f32[64,1024]{0,1:T(8,128)}) %all-reduce.18.cloned.1.call-update) | async-done | bytes 262160 | tf_op jit(solution)/shard_map/psum | solution.py:131
  266.2 7.4 fusion.119
  274.0 33.4 %while.124 = (s32[]{:T(128)}, f32[16,32,128]{2,1,0:T(8,128)S(1)}, s32[]{:T(128)}, f32[16,32,128]{2,1,0:T(8,128)S(1)}, f32[16,32,128]{2,1,0:T(8,128)S(1)}, /*inde...) while((s32[]{:T(128)}, f32[16,32,128]{2,1,0:T(8,128)S(1)}, s32[]{:T(128)}, ...), condition=%wide.region_12.14_spmd, body=%wide.region_11.13_spmd.sunk | while | flops 1048578 | bytes 3340533 | solution.py:86
  276.0 2.4 collective-permute-start.9
  279.5 1.9 collective-permute-start.10
  284.9 3.4 collective-permute-start.9
  289.5 4.8 collective-permute-start.10
  297.2 3.1 collective-permute-start.9
  301.4 4.1 collective-permute-start.10
  307.4 6.7 while.125
  314.8 80.0 %all-reduce.14 = (f32[]{:T(128)}, f32[]{:T(128)}) all-reduce(f32[]{:T(128)} %get-tuple-element.412, f32[]{:T(128)} %get-tuple-element.411), channel_id=1, replica_groups=mesh['lat'=16,'lon'=16] {'lat','lon'}, use_global_device_ids=true, to_apply=%region_5.6 | all-reduce | flops 2 | bytes 16 | tf_op jit(solution)/shard_map/psum | solution.py:127
  396.8 74.5 %psum.45 = f32[]{:T(128)} all-reduce(f32[]{:T(128)} %multiply_reduce_fusion.1), channel_id=1, replica_groups=mesh['lat'=16,'lon'=16] {'lat','lon'}, use_global_device_ids=true, to_apply=%region_18.20 | all-reduce | flops 1 | bytes 8 | tf_op jit(solution)/shard_map/psum | solution.py:140
  473.4 6.7 while.126
  480.1 31.6 %while.127 = (s32[]{:T(128)}, f32[16,32,128]{2,1,0:T(8,128)S(1)}, s32[]{:T(128)}, f32[16,32,128]{2,1,0:T(8,128)S(1)}, f32[16,32,128]{2,1,0:T(8,128)S(1)}, /*inde...) while((s32[]{:T(128)}, f32[16,32,128]{2,1,0:T(8,128)S(1)}, s32[]{:T(128)}, ...), condition=%wide.region_22.24_spmd, body=%wide.region_21.23_spmd.sunk | while | flops 1048578 | bytes 3340533 | solution.py:86
  480.8 3.6 collective-permute-start.13
  485.6 1.7 collective-permute-start.14
  490.4 3.9 collective-permute-start.13
  495.4 3.1 collective-permute-start.14
  500.7 3.8 collective-permute-start.13
  505.6 4.0 collective-permute-start.14
  512.4 11.8 %fusion.120 = f32[192,1,64]{2,1,0:T(1,128)S(1)} fusion(f32[192,128,1]{1,2,0:T(1,128)S(1)} %bitcast.55, f32[192,64,128]{2,1,0:T(8,128)} %param.35), kind=kOutput, calls=%fused_computation.195 | convolution fusion | flops 18874368 | bytes 6438912 | tf_op jit(solution)/shard_map/sok,sk->os/dot_general | solution.py:130
  524.3 1.9 fusion.73
  526.2 114.6 %all-reduce.20.cloned.1.call-done = f32[64,1024]{0,1:T(8,128)} async-done(((f32[64,1024]{0,1:T(8,128)}), f32[64,1024]{0,1:T(8,128)}) %all-reduce.20.cloned.1.call-update) | async-done | bytes 262160 | tf_op jit(solution)/shard_map/psum | solution.py:131
  642.5 7.4 fusion.121
  650.3 33.6 %while.128 = (s32[]{:T(128)}, f32[16,32,128]{2,1,0:T(8,128)S(1)}, s32[]{:T(128)}, f32[16,32,128]{2,1,0:T(8,128)S(1)}, f32[16,32,128]{2,1,0:T(8,128)S(1)}, /*inde...) while((s32[]{:T(128)}, f32[16,32,128]{2,1,0:T(8,128)S(1)}, s32[]{:T(128)}, ...), condition=%wide.region_25.27_spmd, body=%wide.region_24.26_spmd.sunk | while | flops 1048578 | bytes 3340533 | solution.py:86
  652.4 2.4 collective-permute-start.17
  656.0 1.9 collective-permute-start.18
  661.4 3.4 collective-permute-start.17
  665.9 4.8 collective-permute-start.18
  673.6 3.1 collective-permute-start.17
  677.8 4.1 collective-permute-start.18
  683.9 6.7 while.129
  691.3 80.0 %psum.47 = f32[]{:T(128)} all-reduce(f32[]{:T(128)} %get-tuple-element.559), channel_id=1, replica_groups=mesh['lat'=16,'lon'=16] {'lat','lon'}, use_global_device_ids=true, to_apply=%region_29.31 | all-reduce | flops 1 | bytes 8 | tf_op jit(solution)/shard_map/psum | solution.py:134
  773.4 6.7 while.130
  780.1 32.0 %while.131 = (s32[]{:T(128)}, f32[16,32,128]{2,1,0:T(8,128)S(1)}, s32[]{:T(128)}, f32[16,32,128]{2,1,0:T(8,128)S(1)}, f32[16,32,128]{2,1,0:T(8,128)S(1)}, /*inde...) while((s32[]{:T(128)}, f32[16,32,128]{2,1,0:T(8,128)S(1)}, s32[]{:T(128)}, ...), condition=%wide.region_33.35_spmd, body=%wide.region_32.34_spmd.sunk | while | flops 1048578 | bytes 3340533 | solution.py:86
  780.8 3.6 collective-permute-start.21
  785.6 1.8 collective-permute-start.22
  791.3 3.9 collective-permute-start.21
  796.3 2.6 collective-permute-start.22
  801.8 3.5 collective-permute-start.21
  806.3 3.8 collective-permute-start.22
  (363 shorter events, 92.6 us)
Async XLA Ops:
  7.2 257.4 %all-reduce.18.cloned.1.call-start = ((), (), s32[]{:S(2)}) async-start(), calls=%async_computation | async-start | bytes 1048576 | tf_op jit(solution)/shard_map/psum | solution.py:131
  8.0 37.8 %collective-permute-start.24 = (f32[1,32,128]{2,1,0:T(8,128)S(1)}, f32[1,32,128]{2,1,0:T(8,128)S(1)}, u32[]{:S(2)}, u32[]{:S(2)}) collective-permute-start(f32[1,32,128]{2,1,0:T(8,128)S(1)} %get-tuple-element.609), channel_id=1, source_target_pairs={{0,16},{16,32},{32,48},{48,64},{64,80},{80,96},{96,112},{112,128},... | collective-permute-start | bytes 49160 | tf_op jit(solution)/shard_map/ppermute | solution.py:15
  9.3 36.6 %collective-permute-start.25 = (f32[1,32,128]{2,1,0:T(8,128)S(1)}, f32[1,32,128]{2,1,0:T(8,128)S(1)}, u32[]{:S(2)}, u32[]{:S(2)}) collective-permute-start(f32[1,32,128]{2,1,0:T(8,128)S(1)} %get-tuple-element.608), channel_id=1, source_target_pairs={{16,0},{32,16},{48,32},{64,48},{80,64},{96,80},{112,96},{128,112},... | collective-permute-start | bytes 49160 | tf_op jit(solution)/shard_map/ppermute | solution.py:18
  46.0 3.1 collective-permute-start.27
  50.1 4.8 collective-permute-start
  50.2 4.7 collective-permute-start.1
  55.0 3.4 collective-permute-start.2
  57.5 2.4 collective-permute-start.3
  60.8 4.8 collective-permute-start
  60.9 4.7 collective-permute-start.1
  65.7 5.6 collective-permute-start.2
  72.5 5.0 collective-permute-start
  73.4 4.1 collective-permute-start.1
  77.6 4.9 collective-permute-start.2
  97.7 5.1 collective-permute-start.4
  98.9 3.8 collective-permute-start.5
  102.8 4.9 collective-permute-start.6
  108.9 5.1 collective-permute-start.4
  110.1 3.8 collective-permute-start.5
  114.0 4.9 collective-permute-start.6
  120.1 5.1 collective-permute-start.4
  121.4 3.8 collective-permute-start.5
  125.3 4.9 collective-permute-start.6
  146.3 494.5 %all-reduce.20.cloned.1.call-start = ((), (), s32[]{:S(2)}) async-start(), calls=%async_computation.1 | async-start | bytes 1048576 | tf_op jit(solution)/shard_map/psum | solution.py:131
  274.7 4.8 collective-permute-start.8
  276.0 3.5 collective-permute-start.9
  279.5 3.1 collective-permute-start.10
  281.4 2.3 collective-permute-start.11
  284.6 4.8 collective-permute-start.8
  284.9 4.5 collective-permute-start.9
  289.5 5.6 collective-permute-start.10
  296.3 5.0 collective-permute-start.8
  297.2 4.2 collective-permute-start.9
  301.4 4.9 collective-permute-start.10
  480.7 4.8 collective-permute-start.12
  480.8 4.7 collective-permute-start.13
  485.6 3.8 collective-permute-start.14
  487.3 2.1 collective-permute-start.15
  490.3 5.0 collective-permute-start.12
  490.4 5.0 collective-permute-start.13
  495.4 4.0 collective-permute-start.14
  500.5 5.1 collective-permute-start.12
  500.7 4.9 collective-permute-start.13
  505.6 4.9 collective-permute-start.14
  651.1 4.8 collective-permute-start.16
  652.4 3.5 collective-permute-start.17
  656.0 3.1 collective-permute-start.18
  657.9 2.3 collective-permute-start.19
  661.1 4.8 collective-permute-start.16
  661.4 4.5 collective-permute-start.17
  665.9 5.6 collective-permute-start.18
  672.7 5.0 collective-permute-start.16
  673.6 4.2 collective-permute-start.17
  677.8 4.9 collective-permute-start.18
  780.7 4.8 collective-permute-start.20
  780.8 4.7 collective-permute-start.21
  785.6 4.8 collective-permute-start.22
  787.4 3.0 collective-permute-start.23
  791.2 5.0 collective-permute-start.20
  791.3 5.0 collective-permute-start.21
  796.3 4.0 collective-permute-start.22
  801.2 5.1 collective-permute-start.20
  801.8 4.5 collective-permute-start.21
  806.3 4.6 collective-permute-start.22
  (20 other events, 139.6 us)
Sparse Core Ops, SparseCore 0:
  146.4 118.1 all-reduce.17
  526.3 114.4 all-reduce.19
where the time goes:
time: 836 us; the launch traced here: 820 us
  blocking collectives  276 us (33%)
  waiting for transfers between devices  261 us (31%)
  starting transfers between devices  138 us (17%)
  matrix products  54.6 us (7%)
  loops' own time  44.4 us (5%)
  between operations  18.6 us (2%)
  other arithmetic  14.5 us (2%)
  local copies, waits for them, and re-layouts  12.7 us (2%)
    psum x2, waiting for transfers between devices, local(): all_obs = lax.psum(jnp.dot(block_obs, row_hot, precision=highest), 'lon')  214 us
    ppermute x38, starting transfers between devices, extended(): lax.ppermute(lax.slice_in_dim(block, 0, width, axis=dim), axis, backward)  123 us
    psum x1, blocking collectives, local(): norm_now = lax.psum(jnp.sum(residual * residual), ('lat', 'lon'))  80 us
    psum x1, blocking collectives, local(): curvature_sum = lax.psum(jnp.sum(direction * image_vec), ('lat', 'lon'))  80 us
    psum x1, blocking collectives, local(): norm_next = lax.psum(jnp.sum(residual * residual), ('lat', 'lon'))  74.5 us
    ppermute x38, waiting for transfers between devices, extended(): lax.ppermute(lax.slice_in_dim(block, block.shape[dim] - width, None, axis...  27.8 us
    another operation x6, loops' own time, vertical(): lax.fori_loop(0, vertical_count, lambda counter, running: vertical_pass(r...  27.8 us
    dot_general x2, matrix products, local(): block_obs = jnp.einsum('sok,sk->os', jacobian, picked, precision=highest)  23.7 us
  transfers between devices with their start and end apart: 78, of which 55 were waited for; matrix products, arithmetic and copies ran while one was open for 1% of the time, Pallas kernels for 0%

commit v1 on v0

v1 whole, which is shorter than its diff:
```python
import functools

import jax
import jax.numpy as jnp
from jax import lax
from jax.experimental import pallas as pl
from jax.experimental.pallas import tpu as pltpu
from jax.sharding import PartitionSpec as P

MOST = 6
LEAST = 3
SIDE = 8
F32 = jnp.float32
BF16 = jnp.bfloat16
MOVES = tuple((i, j) for i in (-1, 0, 1) for j in (-1, 0, 1) if (i, j) != (0, 0))


def split(value):
    high = value.astype(BF16)
    return high, (value - high.astype(F32)).astype(BF16)


def dot2(left, right):
    high, low = split(left)
    return jnp.dot(high, right, preferred_element_type=F32) + jnp.dot(
        low, right, preferred_element_type=F32
    )


def dot2r(left, right):
    high, low = split(right)
    return jnp.dot(left, high, preferred_element_type=F32) + jnp.dot(
        left, low, preferred_element_type=F32
    )


def kernel(
    shape, counts, cols, rows_in, innov, weight, jac_in, kh_in, kv,
    increment, residual_out,
    jac, kap, ext, tmp, lco, vco, lst, rhot, rhott, chot, contrib,
    grad, resid, evolved, pair_out, pair_in, wide,
    zbuf, zsib, zchip, zin, zown, band, lat_out, lat_in,
    local_sem, halo_s, halo_r, pair_s, pair_r, sib_s, sib_r, rs_s, rs_r,
    ag_s, ag_r, fw_s, fw_r, lat_s, lat_r,
):
    n_lat, n_lon, cells_i, cells_j, levels, slots, obs = shape
    chips = n_lon // 2
    half = obs // 2
    span = cells_j + 2 * SIDE
    total_rows = cells_i + 2 * MOST
    a = lax.axis_index("lat")
    b = lax.axis_index("lon")
    chip = b // 2
    core = lax.rem(b, 2)
    sibling = chip * 2 + 1 - core
    lat_of = lambda d: lax.rem(a + d + n_lat, n_lat)
    lon_of = lambda d: lax.rem(b + d + n_lon, n_lon)
    chip_of = lambda d: lax.rem(chip + d + chips, chips)
    started = []

    def remote(src, dst, ss, rs, to_lat, to_lon):
        copy = pltpu.make_async_remote_copy(
            src_ref=src, dst_ref=dst, send_sem=ss, recv_sem=rs,
            device_id=(to_lat, to_lon), device_id_type=pl.DeviceIdType.MESH,
        )
        copy.start()
        started.append(copy)
        return copy

    rows_src = {-1: slice(MOST, 2 * MOST), 0: slice(MOST, MOST + cells_i), 1: slice(cells_i, cells_i + MOST)}
    rows_dst = {-1: slice(MOST + cells_i, total_rows), 0: slice(MOST, MOST + cells_i), 1: slice(0, MOST)}
    cols_src = {-1: slice(SIDE, 2 * SIDE), 0: slice(SIDE, SIDE + cells_j), 1: slice(cells_j, cells_j + SIDE)}
    cols_dst = {-1: slice(SIDE + cells_j, span), 0: slice(SIDE, SIDE + cells_j), 1: slice(0, SIDE)}

    def halo(ref, which):
        return [
            remote(
                ref.at[rows_src[i], cols_src[j], :], ref.at[rows_dst[i], cols_dst[j], :],
                halo_s.at[which, m], halo_r.at[which, m], lat_of(i), lon_of(j),
            )
            for m, (i, j) in enumerate(MOVES)
        ]

    jac_copy = pltpu.make_async_copy(jac_in, jac, local_sem.at[0])
    jac_copy.start()
    kap_copy = pltpu.make_async_copy(
        kh_in, kap.at[MOST:MOST + cells_i, SIDE:SIDE + cells_j, :], local_sem.at[1]
    )
    kap_copy.start()

    partners = [(lat_of(i), lon_of(j)) for i, j in MOVES]
    partners += [(lat_of(d), b) for d in range(2, n_lat - 1)]
    partners += [(a, chip_of(d) * 2 + core) for d in range(1, chips)]
    partners += [(a, sibling)]
    barrier = pltpu.get_barrier_semaphore()
    for to_lat, to_lon in partners:
        pl.semaphore_signal(
            barrier, inc=1, device_id=(to_lat, to_lon), device_id_type=pl.DeviceIdType.MESH
        )

    pair_out[0] = weight[...] * innov[...]
    pair_out[1] = weight[...]

    lst[...] = jnp.full(lst.shape, n_lon * obs, jnp.int32)
    lst[0:2, 0:slots] = rows_in[...]
    padded = lst.shape[1]
    row_line = lst[0:1, :]
    col_line = lst[1:2, :]
    lane = lax.broadcasted_iota(jnp.int32, (padded, 128), 1)
    row_column = jnp.transpose(jnp.broadcast_to(row_line.astype(F32), (128, padded))).astype(jnp.int32)
    for c in range(chips):
        rhot[:, 128 * c:128 * c + 128] = jnp.where(row_column == lane + 128 * c, 1.0, 0.0).astype(BF16)
    sub = lax.broadcasted_iota(jnp.int32, (128, padded), 0)
    for c in range(chips):
        rhott[128 * c:128 * c + 128, :] = jnp.where(row_line == sub + 128 * c, 1.0, 0.0).astype(BF16)
    for c in range(cells_i * cells_j // 128):
        chot[128 * c:128 * c + 128, :] = jnp.where(
            (col_line == sub + 128 * c) & (row_line < n_lon * obs), 1.0, 0.0
        ).astype(BF16)
    contrib[slots:padded, :] = jnp.zeros((padded - slots, levels), F32)

    pl.semaphore_wait(barrier, len(partners))
    pair = remote(pair_out, pair_in, pair_s, pair_r, a, sibling)
    kap_copy.wait()
    kap_moves = halo(kap, 0)

    level = lax.broadcasted_iota(jnp.int32, (cells_j, levels), 1)

    @pl.loop(0, cells_i)
    def _(i):
        root = jnp.sqrt(kv[i])
        below = jnp.where(level < levels - 1, root * pltpu.roll(root, levels - 1, 1), 0.0)
        above = jnp.where(level > 0, root * pltpu.roll(root, 1, 1), 0.0)
        vco[0, i] = 1.0 - below - above
        vco[1, i] = below
        vco[2, i] = above

    lateral_count = jnp.full((span, levels), counts[0], jnp.int32)
    vertical_count = jnp.full((cells_j, levels), counts[1], jnp.int32)

    def vertical(i, w):
        keep, below, above = vco[0, i], vco[1, i], vco[2, i]
        for p in range(MOST):
            new = keep * w + below * pltpu.roll(w, levels - 1, 1) + above * pltpu.roll(w, 1, 1)
            w = new if p < LEAST else jnp.where(vertical_count > p, new, w)
        return w

    def lateral(field, post):
        source = ext.at[field]
        for p in range(MOST):
            last = p == MOST - 1
            target = tmp.at[p % 2]
            begin = p + 1

            @pl.loop(0, (total_rows - 2 * begin) // 2)
            def _(g, source=source, target=target, p=p, last=last, begin=begin):
                for u in range(2):
                    i = begin + 2 * g + u
                    w = source[i]
                    new = (
                        lco[0, i] * w + lco[1, i] * source[i - 1] + lco[2, i] * source[i + 1]
                        + lco[3, i] * pltpu.roll(w, 1, 0) + lco[4, i] * pltpu.roll(w, span - 1, 0)
                    )
                    if p >= LEAST:
                        new = jnp.where(lateral_count > p, new, w)
                    if last:
                        post(i - MOST, new[SIDE:SIDE + cells_j, :])
                    else:
                        target[i] = new
            source = target

    def put_band(r, piece, tile):
        band[r, core, chip, 0:half, :] = piece
        band[r, core, chip, half:half + 8, :] = tile
        mine = band.at[r, core, chip]
        order = sorted(range(1, chips), key=lambda d: -min(d, chips - d))
        sent = {
            d: remote(mine, mine, ag_s.at[r, d], ag_r.at[r, d], a, chip_of(d) * 2 + core)
            for d in order
        }
        forwards = [remote(mine, mine, fw_s.at[r, 0], fw_r.at[r, 0], a, sibling)]
        for d in reversed(order):
            sent[d].wait_recv()
            arrived = band.at[r, core, chip_of(-d)]
            forwards.append(remote(arrived, arrived, fw_s.at[r, d], fw_r.at[r, d], a, sibling))
        for copy in forwards:
            copy.wait_recv()

    def band_matrix(r):
        return jnp.concatenate(
            [
                jnp.concatenate([band[r, h, c, 0:half, :] for c in range(chips)], axis=1)
                for h in range(2)
            ],
            axis=0,
        )

    def band_tile(r):
        tile = band[r, 0, 0, half:half + 8, :]
        for h in range(2):
            for c in range(chips):
                if h or c:
                    tile = tile + band[r, h, c, half:half + 8, :]
        return tile

    def send_lat(i, tile):
        lat_out[i] = tile
        return [
            remote(lat_out.at[i], lat_in.at[i, d - 1], lat_s.at[i, d - 1], lat_r.at[i, d - 1], lat_of(d), b)
            for d in range(1, n_lat)
        ]

    def sum_lat(i, copies):
        tile = lat_out[i]
        for d, copy in enumerate(copies):
            copy.wait_recv()
            tile = tile + lat_in[i, d]
        return tile

    def adjoint(r, field):
        taken = dot2(band_matrix(r), rhott[...])
        for block in range(0, slots, 128):
            count = min(128, slots - block)
            part = taken[:, block:block + 128]

            def body(g, part, block=block):
                first = pl.multiple_of(block + 8 * g, 8)
                lines = []
                for u in range(8):
                    product = jac[first + u] * jnp.broadcast_to(part[:, u:u + 1], (obs, levels))
                    lines.append(jnp.sum(product, axis=0, keepdims=True))
                contrib[pl.ds(first, 8), :] = jnp.concatenate(lines, axis=0)
                return pltpu.roll(part, 120, 1)

            lax.fori_loop(0, count // 8, body, part)
        columns = dot2r(chot[...], contrib[...])
        for i in range(cells_i):
            ext[field, MOST + i, SIDE:SIDE + cells_j, :] = columns[cells_j * i:cells_j * i + cells_j, :]

    def observe(which, r, tile):
        lane_of = lax.broadcasted_iota(jnp.int32, (obs, 128), 1)
        parts = []
        for block in range(0, slots, 128):
            count = min(128, slots - block)

            def body(g, acc, block=block):
                for u in range(8):
                    s = block + 8 * g + u
                    column = jnp.minimum(cols[1, s], cells_i * cells_j - 1)
                    line = evolved[which, pl.ds(column, 1), :]
                    value = jnp.sum(jac[s] * line, axis=1, keepdims=True)
                    acc = jnp.where(lane_of == 8 * g + u, value, acc)
                return acc

            parts.append(lax.fori_loop(0, count // 8, body, jnp.zeros((obs, 128), F32)))
        partial = dot2(jnp.concatenate(parts, axis=1), rhot[...])
        for h in range(2):
            for c in range(chips):
                zbuf[r, h, c, 0:half, :] = partial[half * h:half * h + half, 128 * c:128 * c + 128]
                zbuf[r, h, c, half:half + 8, :] = tile
        remote(zbuf.at[r, 1 - core], zsib.at[r], sib_s.at[r], sib_r.at[r], a, sibling).wait_recv()
        for c in range(chips):
            zchip[r, c] = zbuf[r, core, c] + zsib[r, c]
        order = sorted(range(1, chips), key=lambda d: -min(d, chips - d))
        copies = [
            remote(
                zchip.at[r, chip_of(d)], zin.at[r, d - 1], rs_s.at[r, d - 1], rs_r.at[r, d - 1],
                a, chip_of(d) * 2 + core,
            )
            for d in order
        ]
        total = zchip[r, chip]
        for copy in copies:
            copy.wait_recv()
        for d in range(1, chips):
            total = total + zin[r, d - 1]
        return total[0:half, :], total[half:half + 8, :]

    def fold(value):
        return jnp.sum(value.reshape(value.shape[0] // 8, 8, levels), axis=0)

    def whole(value):
        return jnp.sum(jnp.sum(value, axis=0, keepdims=True), axis=1, keepdims=True)

    pair.wait_recv()
    for q in range(2):
        own, other = pair_out[q], pair_in[q]
        wide[q] = jnp.concatenate(
            [jnp.where(core == 0, own, other), jnp.where(core == 0, other, own)], axis=1
        )
    offset = pl.multiple_of(core * half, half)
    put_band(0, wide[0, pl.ds(offset, half), :], jnp.zeros((8, levels), F32))
    weight_own = wide[1, pl.ds(offset, half), :]
    jac_copy.wait()
    adjoint(0, 0)
    moves = halo(ext.at[0], 1)

    for copy in kap_moves:
        copy.wait_recv()
    north = jnp.where(a == 0, 0.0, 1.0)
    south = jnp.where(a == n_lat - 1, 0.0, 1.0)
    for i in range(MOST):
        kap[i] = kap[i] * north
        kap[MOST + cells_i + i] = kap[MOST + cells_i + i] * south

    @pl.loop(0, total_rows)
    def _(i):
        tmp[0, i] = jnp.sqrt(kap[i])

    @pl.loop(1, total_rows - 1)
    def _(i):
        root = tmp[0, i]
        up = root * tmp[0, i - 1]
        down = root * tmp[0, i + 1]
        west = root * pltpu.roll(root, 1, 0)
        east = root * pltpu.roll(root, span - 1, 0)
        lco[0, i] = 1.0 - (up + down + west + east)
        lco[1, i] = up
        lco[2, i] = down
        lco[3, i] = west
        lco[4, i] = east

    def wait_halo(copies):
        for copy in copies:
            copy.wait_recv()

    def middle(field, i):
        return ext.at[field, MOST + i, SIDE:SIDE + cells_j, :]

    zero_tile = jnp.zeros((8, levels), F32)
    acc_a = lat_out.at[4]
    acc_b = lat_out.at[5]
    wait_halo(moves)
    acc_a[...] = zero_tile

    def post_gradient(i, w):
        w = vertical(i, w)
        grad[i] = w
        acc_a[...] += fold(w * w)
        ext[1, MOST + i, SIDE:SIDE + cells_j, :] = vertical(i, w)

    lateral(0, post_gradient)
    norm_copies = send_lat(0, acc_a[...])
    wait_halo(halo(ext.at[1], 2))

    def post_evolved(which, i, w):
        evolved[which, pl.ds(pl.multiple_of(i * cells_j, cells_j), cells_j), :] = w

    lateral(1, functools.partial(post_evolved, 0))

    piece, tile = observe(0, 0, sum_lat(0, norm_copies))
    norm = whole(tile)
    zown[...] = piece
    weighted = weight_own * piece
    put_band(1, weighted, fold(weighted * piece))
    curve_copies = send_lat(1, band_tile(1))
    adjoint(1, 2)
    moves = halo(ext.at[2], 3)
    alpha_first = norm / (norm + whole(sum_lat(1, curve_copies)))
    alpha_wide = jnp.broadcast_to(alpha_first, (cells_j, levels))
    wait_halo(moves)
    acc_a[...] = zero_tile
    acc_b[...] = zero_tile

    def post_residual(i, w):
        g = grad[i]
        new = g - alpha_wide * (g + vertical(i, w))
        resid[i] = new
        acc_a[...] += fold(new * new)
        acc_b[...] += fold(new * g)
        ext[3, MOST + i, SIDE:SIDE + cells_j, :] = vertical(i, new)

    lateral(2, post_residual)
    sub8 = lax.broadcasted_iota(jnp.int32, (8, levels), 0)
    norm_copies = send_lat(
        2,
        jnp.where(
            sub8 == 0,
            jnp.sum(acc_a[...], axis=0, keepdims=True),
            jnp.where(sub8 == 1, jnp.sum(acc_b[...], axis=0, keepdims=True), 0.0),
        ),
    )
    wait_halo(halo(ext.at[3], 4))
    lateral(3, functools.partial(post_evolved, 1))

    piece, tile = observe(1, 1, sum_lat(2, norm_copies))
    norm_next = jnp.sum(tile[0:1, :], axis=1, keepdims=True)
    cross = jnp.sum(tile[1:2, :], axis=1, keepdims=True)
    beta = norm_next / norm
    square = norm_next + 2.0 * beta * cross + beta * beta * norm
    piece = piece + beta * zown[...]
    weighted = weight_own * piece
    put_band(2, weighted, fold(weighted * piece))
    curve_copies = send_lat(3, band_tile(2))
    adjoint(2, 4)
    moves = halo(ext.at[4], 5)
    alpha_second = norm_next / (square + whole(sum_lat(3, curve_copies)))
    second_wide = jnp.broadcast_to(alpha_second, (cells_j, levels))
    beta_wide = jnp.broadcast_to(beta, (cells_j, levels))
    wait_halo(moves)

    def post_last(i, w):
        r = resid[i]
        residual_out[i] = r - second_wide * (r + beta_wide * grad[i] + vertical(i, w))
        place = pl.ds(pl.multiple_of(i * cells_j, cells_j), cells_j)
        first, second = evolved[0, place, :], evolved[1, place, :]
        increment[i] = alpha_wide * first + second_wide * (second + beta_wide * first)

    lateral(4, post_last)
    for copy in started:
        copy.wait_send()


def local(n_lat, n_lon, innovation, obs_weight, jacobian, block_list, pass_counts, kappa_h, kappa_v):
    cells_i, cells_j, levels = kappa_h.shape
    slots, obs, _ = jacobian.shape
    shape = (n_lat, n_lon, cells_i, cells_j, levels, slots, obs)
    chips = n_lon // 2
    half = obs // 2
    span = cells_j + 2 * SIDE
    total_rows = cells_i + 2 * MOST
    padded = -(-slots // 128) * 128
    columns = cells_i * cells_j
    vmem = pltpu.VMEM
    dma = pltpu.SemaphoreType.DMA
    field = jax.ShapeDtypeStruct((cells_i, cells_j, levels), F32)
    in_vmem = pl.BlockSpec(memory_space=pltpu.VMEM)
    in_smem = pl.BlockSpec(memory_space=pltpu.SMEM)
    in_any = pl.BlockSpec(memory_space=pl.ANY)
    return pl.pallas_call(
        functools.partial(kernel, shape),
        out_shape=(field, field),
        in_specs=[in_smem, in_smem, in_vmem, in_vmem, in_vmem, in_any, in_any, in_vmem],
        out_specs=(in_vmem, in_vmem),
        scratch_shapes=[
            vmem((slots, obs, levels), F32),
            vmem((total_rows, span, levels), F32),
            vmem((5, total_rows, span, levels), F32),
            vmem((2, total_rows, span, levels), F32),
            vmem((5, total_rows, span, levels), F32),
            vmem((3, cells_i, cells_j, levels), F32),
            vmem((8, padded), jnp.int32),
            vmem((padded, 128 * chips), BF16),
            vmem((128 * chips, padded), BF16),
            vmem((columns, padded), BF16),
            vmem((padded, levels), F32),
            vmem((cells_i, cells_j, levels), F32),
            vmem((cells_i, cells_j, levels), F32),
            vmem((2, columns, levels), F32),
            vmem((2, obs, obs), F32),
            vmem((2, obs, obs), F32),
            vmem((2, obs, 2 * obs), F32),
            vmem((2, 2, chips, half + 8, 128), F32),
            vmem((2, chips, half + 8, 128), F32),
            vmem((2, chips, half + 8, 128), F32),
            vmem((2, chips - 1, half + 8, 128), F32),
            vmem((half, 128), F32),
            vmem((3, 2, chips, half + 8, 128), F32),
            vmem((6, 8, 128), F32),
            vmem((4, n_lat - 1, 8, 128), F32),
            dma((2,)),
            dma((6, 8)), dma((6, 8)),
            dma, dma,
            dma((2,)), dma((2,)),
            dma((2, chips - 1)), dma((2, chips - 1)),
            dma((3, chips)), dma((3, chips)),
            dma((3, chips)), dma((3, chips)),
            dma((4, n_lat - 1)), dma((4, n_lat - 1)),
        ],
        compiler_params=pltpu.CompilerParams(
            collective_id=0, has_side_effects=True, vmem_limit_bytes=60 * 1024 * 1024
        ),
    )(pass_counts, block_list, block_list, innovation, obs_weight, jacobian, kappa_h, kappa_v)


def solution(mesh):
    return jax.shard_map(
        functools.partial(local, mesh.shape["lat"], mesh.shape["lon"]),
        mesh=mesh,
        in_specs=(
            P(None, ("lat", "lon")),
            P(None, ("lat", "lon")),
            P(("lat", "lon"), None, None),
            P(None, ("lat", "lon")),
            P(),
            P("lat", "lon", None),
            P("lat", "lon", None),
        ),
        out_specs=(P("lat", "lon", None), P("lat", "lon", None)),
        check_vma=False,
    )
```

time: 836 us -> 140 us (0.17)
  the two profiles are of different devices: /device:TPU:9 before, /device:TPU:1 now
where the time goes in v1:
time: 140 us
  Pallas kernels  136 us (97%)
  local copies, waits for them, and re-layouts  3.34 us (2%)
    pallas_call x1, Pallas kernels, local(): pl.pallas_call(functools.partial(kernel, shape), out_shape=(field, field)...  136 us
    unnamed x2, local copies, waits for them, and re-layouts  3.34 us

profile of v1, /device:TPU:1, one launch (start us, length us, event | category | flops | bytes accessed | tf_op | source)
XLA Modules:
  0.0 139.6 jit_solution(9538430666038520185)
XLA Ops:
  0.6 135.6 %shard_map.86 = (f32[16,32,128]{2,1,0:T(8,128)}, f32[16,32,128]{2,1,0:T(8,128)}) custom-call(s32[2]{0:T(128)} %counts.1, s32[2,192]{1,0:T(2,128)} %rows_in.1, s32[2,192]{1,0:T(2,128)} %rows_in.1, f32[64,64]{1,0:T(8,128)} %innov.1, f32[64,64]{1,0:T(8,128)} %weight.1, f32[192,64,128]{2,1,0:T(8,128)} %jac_in.1, f32[16,32,128]{2,1,0:T(8,128)} %kh_in.1, ...), custom_call_target="tpu_custom_call" | custom-call | tf_op jit(solution)/shard_map/pallas_call | solution.py:430
  136.2 1.7 %copy.11 = f32[16,32,128]{2,1,0:T(8,128)} copy(f32[16,32,128]{2,1,0:T(8,128)} %get-tuple-element.4) | data formatting | bytes 524288
  137.9 1.7 %copy.12 = f32[16,32,128]{2,1,0:T(8,128)} copy(f32[16,32,128]{2,1,0:T(8,128)} %get-tuple-element.5) | data formatting | bytes 524288

commit v2 on v1

v2 whole, which is shorter than its diff:
```python
import functools

import jax
import jax.numpy as jnp
from jax import lax
from jax.experimental import pallas as pl
from jax.experimental.pallas import tpu as pltpu
from jax.sharding import PartitionSpec as P

MOST = 6
LEAST = 3
SIDE = 8
F32 = jnp.float32
BF16 = jnp.bfloat16
MOVES = tuple((i, j) for i in (-1, 0, 1) for j in (-1, 0, 1) if (i, j) != (0, 0))


def split(value):
    high = value.astype(BF16)
    return high, (value - high.astype(F32)).astype(BF16)


def pick(table, value):
    both = jnp.concatenate(split(value), axis=1)
    out = jnp.dot(table, both, preferred_element_type=F32)
    width = value.shape[1]
    return out[:, :width], out[:, width:]


def kernel(
    shape, counts, rows_in, innov, weight, jac_in, kh_in, kv,
    increment, residual_out,
    jac, jparts, jturn, kap, ext, tmp, lco, vco, lst, rsel, rselt, chot, chott, lhs, contrib, observed,
    done, grad, resid, evolved, square,
    zbuf, zsib, zchip, zin, zown, wown, band, sum_out, sum_in,
    local_sem, halo_s, halo_r, sib_s, sib_r, rs_s, rs_r,
    ag_s, ag_r, fw_s, fw_r, sum_s, sum_r,
):
    n_lat, n_lon, cells_i, cells_j, levels, slots, obs = shape
    chips = n_lon // 2
    half = obs // 2
    span = cells_j + 2 * SIDE
    total_rows = cells_i + 2 * MOST
    columns = cells_i * cells_j
    a = lax.axis_index("lat")
    b = lax.axis_index("lon")
    chip = b // 2
    core = lax.rem(b, 2)
    sibling = chip * 2 + 1 - core
    lat_of = lambda d: lax.rem(a + d + n_lat, n_lat)
    lon_of = lambda d: lax.rem(b + d + n_lon, n_lon)
    chip_of = lambda d: lax.rem(chip + d + chips, chips)
    started = []

    def describe(src, dst, ss, rs, to_lat, to_lon):
        return pltpu.make_async_remote_copy(
            src_ref=src, dst_ref=dst, send_sem=ss, recv_sem=rs,
            device_id=(to_lat, to_lon), device_id_type=pl.DeviceIdType.MESH,
        )

    def remote(*args):
        copy = describe(*args)
        copy.start()
        started.append(copy)
        return copy

    rows_src = {-1: slice(MOST, 2 * MOST), 0: slice(MOST, MOST + cells_i), 1: slice(cells_i, cells_i + MOST)}
    rows_dst = {-1: slice(MOST + cells_i, total_rows), 0: slice(MOST, MOST + cells_i), 1: slice(0, MOST)}
    cols_src = {-1: slice(SIDE, 2 * SIDE), 0: slice(SIDE, SIDE + cells_j), 1: slice(cells_j, cells_j + SIDE)}
    cols_dst = {-1: slice(SIDE + cells_j, span), 0: slice(SIDE, SIDE + cells_j), 1: slice(0, SIDE)}
    sends = {-1: a > 0, 1: a < n_lat - 1}
    gets = {-1: a < n_lat - 1, 1: a > 0}

    def halo_copy(ref, which, m):
        i, j = MOVES[m]
        return describe(
            ref.at[rows_src[i], cols_src[j], :], ref.at[rows_dst[i], cols_dst[j], :],
            halo_s.at[which, m], halo_r.at[which, m], lat_of(i), lon_of(j),
        )

    def halo_send(ref, which, toward):
        picked = [m for m in range(len(MOVES)) if MOVES[m][0] == toward]

        def start():
            for m in picked:
                halo_copy(ref, which, m).start()

        if toward:
            pl.when(sends[toward])(start)
        else:
            start()

    def halo(ref, which):
        for toward in (-1, 1, 0):
            halo_send(ref, which, toward)

    def halo_wait(ref, which, toward, sent=False):
        picked = [m for m in range(len(MOVES)) if MOVES[m][0] == toward]

        def wait():
            for m in picked:
                copy = halo_copy(ref, which, m)
                if sent:
                    copy.wait_send()
                else:
                    copy.wait_recv()

        if toward:
            pl.when((sends if sent else gets)[toward])(wait)
        else:
            wait()

    pieces = local_sem.shape[0] - 1
    chunk = slots // pieces
    jac_copies = [
        pltpu.make_async_copy(
            jac_in.at[q * chunk:(q + 1) * chunk], jac.at[q * chunk:(q + 1) * chunk], local_sem.at[q]
        )
        for q in range(pieces)
    ]
    kap_copy = pltpu.make_async_copy(
        kh_in, kap.at[MOST:MOST + cells_i, SIDE:SIDE + cells_j, :], local_sem.at[pieces]
    )
    kap_copy.start()
    for copy in jac_copies:
        copy.start()

    partners = [(lat_of(i), lon_of(j)) for i, j in MOVES if i and j]
    partners += [(lat_of(d), b) for d in range(1, n_lat)]
    partners += [(a, lon_of(d)) for d in range(1, n_lon)]
    barrier = pltpu.get_barrier_semaphore()
    for to_lat, to_lon in partners:
        pl.semaphore_signal(
            barrier, inc=1, device_id=(to_lat, to_lon), device_id_type=pl.DeviceIdType.MESH
        )

    @pl.when(a == 0)
    def _():
        kap[0:MOST] = jnp.zeros((MOST, span, levels), F32)
        for field in range(5):
            ext[field, 0:MOST] = jnp.zeros((MOST, span, levels), F32)

    @pl.when(a == n_lat - 1)
    def _():
        kap[MOST + cells_i:] = jnp.zeros((MOST, span, levels), F32)
        for field in range(5):
            ext[field, MOST + cells_i:] = jnp.zeros((MOST, span, levels), F32)

    def packed(value):
        square[0:obs, 0:obs] = value
        turned = jnp.transpose(square[...])[0:obs, 0:obs]
        return jnp.concatenate([turned[0:half], turned[half:obs]], axis=1)

    square[...] = jnp.zeros(square.shape, F32)
    wown[...] = packed(weight[...])
    band[0, core, chip] = wown[...] * packed(innov[...])

    pl.semaphore_wait(barrier, len(partners))
    kap_copy.wait()
    order = sorted(range(1, chips), key=lambda d: -min(d, chips - d))

    def send_band(r):
        mine = band.at[r, core, chip]
        sent = {
            d: remote(mine, mine, ag_s.at[r, d], ag_r.at[r, d], a, chip_of(d) * 2 + core)
            for d in order
        }
        return sent, [remote(mine, mine, fw_s.at[r, 0], fw_r.at[r, 0], a, sibling)]

    def wait_band(r, sent, forwards):
        for d in reversed(order):
            sent[d].wait_recv()
            arrived = band.at[r, core, chip_of(-d)]
            forwards.append(remote(arrived, arrived, fw_s.at[r, d], fw_r.at[r, d], a, sibling))
        for copy in forwards:
            copy.wait_recv()

    gathering = send_band(0)
    halo(kap, 0)

    lst[...] = jnp.full(lst.shape, n_lon * obs, jnp.int32)
    lst[0:2, 0:slots] = rows_in[...]
    padded = lst.shape[1]
    row_line = lst[0:1, :]
    col_line = lst[1:2, :]

    def upright(line):
        return jnp.transpose(jnp.broadcast_to(line.astype(F32), (128, padded))).astype(jnp.int32)

    def hot(test):
        return jnp.where(test, 1.0, 0.0).astype(BF16)

    lane = lax.broadcasted_iota(jnp.int32, (padded, 128), 1)
    sub = lax.broadcasted_iota(jnp.int32, (128, padded), 0)
    row_column = upright(row_line)
    col_column = upright(col_line)
    for j in range(2):
        for q in range(n_lon * half // 128):
            place = slice(128 * q, 128 * q + 128)
            rsel[j, :, place] = hot(row_column == 256 * q + half * j + obs * (lane // half) + lane % half)
            rselt[j, place, :] = hot(row_line == 256 * q + half * j + obs * (sub // half) + sub % half)
    for q in range(columns // 128):
        place = slice(128 * q, 128 * q + 128)
        chot[place, :] = hot((col_line == sub + 128 * q) & (row_line < n_lon * obs))
        chott[:, place] = hot(col_column == lane + 128 * q)
    contrib[slots:padded, :] = jnp.zeros((padded - slots, levels), F32)
    observed[slots:padded, :] = jnp.zeros((padded - slots, 128), F32)

    for q, copy in enumerate(jac_copies):
        copy.wait()

        @pl.loop(q * chunk // 4, (q + 1) * chunk // 4)
        def _(g):
            block = jac[pl.ds(4 * g, 4)].reshape(4 * obs, levels)
            place = pl.ds(pl.multiple_of(4 * obs * g, 4 * obs), 4 * obs)
            turned = pl.ds(pl.multiple_of(levels * g, levels), levels)
            jparts[0, place, :], jparts[1, place, :] = split(block)
            jturn[0, turned, :], jturn[1, turned, :] = split(jnp.transpose(block))

    level = lax.broadcasted_iota(jnp.int32, (cells_j, levels), 1)

    @pl.loop(0, cells_i)
    def _(i):
        root = jnp.sqrt(kv[i])
        below = jnp.where(level < levels - 1, root * pltpu.roll(root, levels - 1, 1), 0.0)
        above = jnp.where(level > 0, root * pltpu.roll(root, 1, 1), 0.0)
        vco[0, i] = 1.0 - below - above
        vco[1, i] = below
        vco[2, i] = above

    lateral_count = jnp.full((span, levels), counts[0], jnp.int32)
    vertical_count = jnp.full((cells_j, levels), counts[1], jnp.int32)

    def vertical(rows, values):
        for p in range(MOST):
            news = [
                vco[0, i] * w + vco[1, i] * pltpu.roll(w, levels - 1, 1) + vco[2, i] * pltpu.roll(w, 1, 1)
                for i, w in zip(rows, values)
            ]
            values = news if p < LEAST else [
                jnp.where(vertical_count > p, new, w) for new, w in zip(news, values)
            ]
        return values

    def lateral(field, target):
        def rows_of(p, rows):
            source = ext.at[field] if p == 0 else tmp.at[p - 1]
            news = []
            for i in rows:
                w = source[i]
                new = (
                    lco[0, i] * w + lco[1, i] * source[i - 1] + lco[2, i] * source[i + 1]
                    + lco[3, i] * pltpu.roll(w, 1, 0) + lco[4, i] * pltpu.roll(w, span - 1, 0)
                )
                news.append(new if p < LEAST else jnp.where(lateral_count > p, new, w))
            for i, new in zip(rows, news):
                if p < MOST - 1:
                    tmp[p, i] = new
                else:
                    place = (i - MOST) * cells_j
                    if not isinstance(place, int):
                        place = pl.multiple_of(place, cells_j)
                    target[pl.ds(place, cells_j), :] = new[SIDE:SIDE + cells_j, :]

        halo_wait(ext.at[field], field + 1, 0)
        for p in range(MOST):
            first = MOST + p + 1

            @pl.loop(0, (cells_i - 2 * p - 2) // 2)
            def _(g, p=p, first=first):
                rows_of(p, [first + 2 * g, first + 2 * g + 1])

        halo_wait(ext.at[field], field + 1, -1)
        halo_wait(ext.at[field], field + 1, 1)
        for p in range(MOST):
            top = p + 1
            low = MOST + cells_i - p - 1

            @pl.loop(0, MOST // 2)
            def _(g, p=p, top=top, low=low):
                rows_of(p, [top + 2 * g, top + 2 * g + 1, low + 2 * g, low + 2 * g + 1])

    def send_sum(i, tile, along_lat):
        sum_out[i] = tile
        count = n_lat if along_lat else n_lon
        return [
            remote(
                sum_out.at[i], sum_in.at[i, d - 1], sum_s.at[i, d - 1], sum_r.at[i, d - 1],
                lat_of(d) if along_lat else a, b if along_lat else lon_of(d),
            )
            for d in range(1, count)
        ]

    def take_sum(i, copies):
        for copy in copies:
            copy.wait_recv()
        tile = sum_out[i]
        for d in range(len(copies)):
            tile = tile + sum_in[i, d]
        return tile

    side8 = lax.broadcasted_iota(jnp.int32, (padded, 128), 0)
    lane8 = lax.broadcasted_iota(jnp.int32, (padded, 128), 1)
    quarter = side8 % 4
    left_block = lane8 // obs == quarter
    right_block = lane8 // obs + 2 == quarter
    first_half = side8 % 8 < 4
    low_lanes = lane8 < obs

    def put_lhs(part, left, right):
        lhs[part, :, 0:128] = left[0:slots]
        lhs[part, :, 128:256] = right[0:slots]

    def natural(part, g):
        first = 8 * obs * g
        return jnp.concatenate(
            [jparts[part, first:first + 4 * obs, :], jparts[part, first + 4 * obs:first + 8 * obs, :]],
            axis=1,
        )

    def turned(part, g):
        return jturn[part, 2 * levels * g:2 * levels * (g + 1), :]

    def products(matrix, finish):
        for g in range(slots // 8):
            place = slice(8 * g, 8 * g + 8)
            left = jnp.concatenate([lhs[0, place, :], lhs[1, place, :]], axis=0).astype(BF16)
            out = sum(jnp.dot(left, matrix(part, g), preferred_element_type=F32) for part in range(2))
            finish(place, out[0:8] + out[8:16])

    def adjoint(r, field):
        values = jnp.concatenate(
            [band[r, k, c] for c in range(chips) for k in range(2)], axis=0
        )
        picked = [pick(rsel[j], values) for j in range(2)]
        for part in range(2):
            taken = jnp.where(low_lanes, picked[0][part], picked[1][part])
            taken = taken + pltpu.roll(taken, obs, 1)
            put_lhs(part, jnp.where(left_block, taken, 0.0), jnp.where(right_block, taken, 0.0))

        def finish(place, out):
            contrib[place, :] = jnp.where(first_half[0:8], out[:, 0:128], out[:, 128:256])

        products(natural, finish)
        high, low = pick(chot[...], contrib[...])
        cells = high + low
        for i in range(cells_i):
            ext[field, MOST + i, SIDE:SIDE + cells_j, :] = cells[cells_j * i:cells_j * i + cells_j, :]

    def observe(which, r):
        picked = pick(chott[...], evolved[which])
        for part in range(2):
            put_lhs(part, jnp.where(first_half, picked[part], 0.0), jnp.where(first_half, 0.0, picked[part]))

        def finish(place, out):
            value = jnp.where(left_block[0:8], out[:, 0:128], 0.0) + jnp.where(
                right_block[0:8], out[:, 128:256], 0.0
            )
            observed[place, :] = value + pltpu.roll(value, obs, 1)

        products(turned, finish)
        high, low = zip(*(pick(rselt[j], observed[...]) for j in range(2)))
        narrow = lax.broadcasted_iota(jnp.int32, high[0].shape, 1) < obs
        partial = jnp.where(narrow, high[0] + low[0], high[1] + low[1])
        for c in range(chips):
            for k in range(2):
                first = half * (2 * c + k)
                zbuf[r, k, c] = partial[first:first + half, :]
        remote(zbuf.at[r, 1 - core], zsib.at[r], sib_s.at[r], sib_r.at[r], a, sibling).wait_recv()
        for c in range(chips):
            zchip[r, c] = zbuf[r, core, c] + zsib[r, c]
        copies = [
            remote(
                zchip.at[r, chip_of(d)], zin.at[r, d - 1], rs_s.at[r, d - 1], rs_r.at[r, d - 1],
                a, chip_of(d) * 2 + core,
            )
            for d in order
        ]
        total = zchip[r, chip]
        for copy in copies:
            copy.wait_recv()
        for d in range(1, chips):
            total = total + zin[r, d - 1]
        return total

    def fold(value):
        return jnp.sum(value.reshape(value.shape[0] // 8, 8, levels), axis=0)

    def whole(value):
        return jnp.sum(jnp.sum(value, axis=0, keepdims=True), axis=1, keepdims=True)

    def two_rows(first, second):
        sub8 = lax.broadcasted_iota(jnp.int32, (8, levels), 0)
        return jnp.where(
            sub8 == 0,
            jnp.sum(first, axis=0, keepdims=True),
            jnp.where(sub8 == 1, jnp.sum(second, axis=0, keepdims=True), 0.0),
        )

    wait_band(0, *gathering)
    adjoint(0, 0)
    halo(ext.at[0], 1)

    for toward in (-1, 0, 1):
        halo_wait(kap, 0, toward)

    @pl.loop(0, total_rows // 2)
    def _(g):
        for u in range(2):
            tmp[0, 2 * g + u] = jnp.sqrt(kap[2 * g + u])

    @pl.loop(0, total_rows // 2 - 1)
    def _(g):
        for u in range(2):
            i = 2 * g + 1 + u
            root = tmp[0, i]
            up = root * tmp[0, i - 1]
            down = root * tmp[0, i + 1]
            west = root * pltpu.roll(root, 1, 0)
            east = root * pltpu.roll(root, span - 1, 0)
            lco[0, i] = 1.0 - (up + down + west + east)
            lco[1, i] = up
            lco[2, i] = down
            lco[3, i] = west
            lco[4, i] = east

    def row(ref, i):
        return ref[i * cells_j:(i + 1) * cells_j, :]

    def middle(field, i, value):
        ext[field, MOST + i, SIDE:SIDE + cells_j, :] = value

    GROUP = 8
    groups = [list(range(q, q + GROUP)) for q in range(0, cells_i, GROUP)]

    def spread_and_send(field, work):
        accs = None
        for q, rows in enumerate(groups):
            parts = work(rows)
            accs = parts if accs is None else [x + y for x, y in zip(accs, parts)]
            if q == 0:
                halo_send(ext.at[field], field + 1, -1)
        halo_send(ext.at[field], field + 1, 1)
        halo_send(ext.at[field], field + 1, 0)
        return accs

    lateral(0, done)

    def gradient_rows(rows):
        ws = vertical(rows, [row(done, i) for i in rows])
        total = sum(fold(w * w) for w in ws)
        nexts = vertical(rows, ws)
        for i, w, following in zip(rows, ws, nexts):
            grad[i] = w
            middle(1, i, following)
        return [total]

    (total,) = spread_and_send(1, gradient_rows)
    norm_lat = send_sum(0, total, True)
    lateral(1, evolved.at[0])
    norm_lon = send_sum(1, take_sum(0, norm_lat), False)

    piece = observe(0, 0)
    zown[...] = piece
    weighted = wown[...] * piece
    band[1, core, chip] = weighted
    gathering = send_band(1)
    curve_lat = send_sum(2, fold(weighted * piece), True)
    norm = whole(take_sum(1, norm_lon))
    wait_band(1, *gathering)
    adjoint(1, 2)
    halo(ext.at[2], 3)
    curve_lon = send_sum(3, take_sum(2, curve_lat), False)
    lateral(2, done)
    alpha_first = norm / (norm + whole(take_sum(3, curve_lon)))
    alpha_wide = jnp.broadcast_to(alpha_first, (cells_j, levels))

    def residual_rows(rows):
        ws = vertical(rows, [row(done, i) for i in rows])
        gs = [grad[i] for i in rows]
        news = [g - alpha_wide * (g + w) for g, w in zip(gs, ws)]
        squares = sum(fold(new * new) for new in news)
        crosses = sum(fold(new * g) for new, g in zip(news, gs))
        nexts = vertical(rows, news)
        for i, new, following in zip(rows, news, nexts):
            resid[i] = new
            middle(3, i, following)
        return [squares, crosses]

    squares, crosses = spread_and_send(3, residual_rows)
    norm_lat = send_sum(4, two_rows(squares, crosses), True)
    lateral(3, evolved.at[1])
    norm_lon = send_sum(5, take_sum(4, norm_lat), False)

    piece = observe(1, 1)
    tile = take_sum(5, norm_lon)
    norm_next = jnp.sum(tile[0:1, :], axis=1, keepdims=True)
    cross = jnp.sum(tile[1:2, :], axis=1, keepdims=True)
    beta = norm_next / norm
    self_product = norm_next + 2.0 * beta * cross + beta * beta * norm
    piece = piece + beta * zown[...]
    weighted = wown[...] * piece
    band[2, core, chip] = weighted
    gathering = send_band(2)
    curve_lat = send_sum(6, fold(weighted * piece), True)
    wait_band(2, *gathering)
    adjoint(2, 4)
    halo(ext.at[4], 5)
    curve_lon = send_sum(7, take_sum(6, curve_lat), False)
    lateral(4, done)
    alpha_second = norm_next / (self_product + whole(take_sum(7, curve_lon)))
    second_wide = jnp.broadcast_to(alpha_second, (cells_j, levels))
    beta_wide = jnp.broadcast_to(beta, (cells_j, levels))
    for rows in groups:
        ws = vertical(rows, [row(done, i) for i in rows])
        for i, w in zip(rows, ws):
            r = resid[i]
            residual_out[i] = r - second_wide * (r + beta_wide * grad[i] + w)
            first, second = row(evolved.at[0], i), row(evolved.at[1], i)
            increment[i] = alpha_wide * first + second_wide * (second + beta_wide * first)

    for copy in started:
        copy.wait_send()
    for which in range(6):
        ref = kap if which == 0 else ext.at[which - 1]
        for toward in (-1, 0, 1):
            halo_wait(ref, which, toward, sent=True)


def local(n_lat, n_lon, innovation, obs_weight, jacobian, block_list, pass_counts, kappa_h, kappa_v):
    cells_i, cells_j, levels = kappa_h.shape
    slots, obs, _ = jacobian.shape
    shape = (n_lat, n_lon, cells_i, cells_j, levels, slots, obs)
    chips = n_lon // 2
    half = obs // 2
    span = cells_j + 2 * SIDE
    total_rows = cells_i + 2 * MOST
    padded = -(-slots // 128) * 128
    columns = cells_i * cells_j
    peers = max(n_lat, n_lon) - 1
    vmem = pltpu.VMEM
    dma = pltpu.SemaphoreType.DMA
    field = jax.ShapeDtypeStruct((cells_i, cells_j, levels), F32)
    in_vmem = pl.BlockSpec(memory_space=pltpu.VMEM)
    in_smem = pl.BlockSpec(memory_space=pltpu.SMEM)
    in_any = pl.BlockSpec(memory_space=pl.ANY)
    return pl.pallas_call(
        functools.partial(kernel, shape),
        out_shape=(field, field),
        in_specs=[in_smem, in_vmem, in_vmem, in_vmem, in_any, in_any, in_vmem],
        out_specs=(in_vmem, in_vmem),
        scratch_shapes=[
            vmem((slots, obs, levels), F32),
            vmem((2, slots * obs, levels), BF16),
            vmem((2, slots // 4 * levels, 4 * obs), BF16),
            vmem((total_rows, span, levels), F32),
            vmem((5, total_rows, span, levels), F32),
            vmem((MOST - 1, total_rows, span, levels), F32),
            vmem((5, total_rows, span, levels), F32),
            vmem((3, cells_i, cells_j, levels), F32),
            vmem((8, padded), jnp.int32),
            vmem((2, padded, half * n_lon), BF16),
            vmem((2, half * n_lon, padded), BF16),
            vmem((columns, padded), BF16),
            vmem((padded, columns), BF16),
            vmem((2, slots, 256), F32),
            vmem((padded, levels), F32),
            vmem((padded, 128), F32),
            vmem((columns, levels), F32),
            vmem((cells_i, cells_j, levels), F32),
            vmem((cells_i, cells_j, levels), F32),
            vmem((2, columns, levels), F32),
            vmem((128, 128), F32),
            vmem((2, 2, chips, half, 128), F32),
            vmem((2, chips, half, 128), F32),
            vmem((2, chips, half, 128), F32),
            vmem((2, chips - 1, half, 128), F32),
            vmem((half, 128), F32),
            vmem((half, 128), F32),
            vmem((3, 2, chips, half, 128), F32),
            vmem((8, 8, 128), F32),
            vmem((8, peers, 8, 128), F32),
            dma((5,)),
            dma((6, 8)), dma((6, 8)),
            dma((2,)), dma((2,)),
            dma((2, chips - 1)), dma((2, chips - 1)),
            dma((3, chips)), dma((3, chips)),
            dma((3, chips)), dma((3, chips)),
            dma((8, peers)), dma((8, peers)),
        ],
        compiler_params=pltpu.CompilerParams(
            collective_id=0, has_side_effects=True, vmem_limit_bytes=60 * 1024 * 1024
        ),
    )(pass_counts, block_list, innovation, obs_weight, jacobian, kappa_h, kappa_v)


def solution(mesh):
    return jax.shard_map(
        functools.partial(local, mesh.shape["lat"], mesh.shape["lon"]),
        mesh=mesh,
        in_specs=(
            P(None, ("lat", "lon")),
            P(None, ("lat", "lon")),
            P(("lat", "lon"), None, None),
            P(None, ("lat", "lon")),
            P(),
            P("lat", "lon", None),
            P("lat", "lon", None),
        ),
        out_specs=(P("lat", "lon", None), P("lat", "lon", None)),
        check_vma=False,
    )
```

time: 140 us -> 102 us (0.73)
  the two profiles are of different devices: /device:TPU:1 before, /device:TPU:9 now
where the time goes in v2:
time: 102 us; the launch traced here: 101 us
  Pallas kernels  96.9 us (95%)
  local copies, waits for them, and re-layouts  3.34 us (3%)
    pallas_call x1, Pallas kernels, local(): pl.pallas_call(functools.partial(kernel, shape), out_shape=(field, field)...  96.9 us
    unnamed x2, local copies, waits for them, and re-layouts  3.34 us

profile of v2, /device:TPU:9, one launch (start us, length us, event | category | flops | bytes accessed | tf_op | source)
XLA Modules:
  0.0 100.9 jit_solution(6960663825688684393)
XLA Ops:
  0.6 96.9 %shard_map.86 = (f32[16,32,128]{2,1,0:T(8,128)}, f32[16,32,128]{2,1,0:T(8,128)}) custom-call(s32[2]{0:T(128)} %counts.1, s32[2,192]{1,0:T(2,128)} %rows_in.1, f32[64,64]{1,0:T(8,128)} %innov.1, f32[64,64]{1,0:T(8,128)} %weight.1, f32[192,64,128]{2,1,0:T(8,128)} %jac_in.1, f32[16,32,128]{2,1,0:T(8,128)} %kh_in.1, f32[16,32,128]{2,1,0:T(8,128)} %kv.1), custom_call_target="tpu_custom_call" | custom-call | tf_op jit(solution)/shard_map/pallas_call | solution.py:547
  97.5 1.7 %copy.11 = f32[16,32,128]{2,1,0:T(8,128)} copy(f32[16,32,128]{2,1,0:T(8,128)} %get-tuple-element.4) | data formatting | bytes 524288
  99.2 1.7 %copy.12 = f32[16,32,128]{2,1,0:T(8,128)} copy(f32[16,32,128]{2,1,0:T(8,128)} %get-tuple-element.5) | data formatting | bytes 524288

commit v3 on v2

--- a/solution.py
+++ b/solution.py
@@ -28,10 +28,10 @@
 
 
 def kernel(
-    shape, counts, rows_in, innov, weight, jac_in, kh_in, kv,
+    shape, counts, rows_hbm, innov_hbm, weight_hbm, jac_in, kh_in, kv_hbm,
     increment, residual_out,
-    jac, jparts, jturn, kap, ext, tmp, lco, vco, lst, rsel, rselt, chot, chott, lhs, contrib, observed,
-    done, grad, resid, evolved, square,
+    rows_in, innov, weight, kv, jac, jparts, jturn, kap, ext, tmp, lco, vco, lst, rsel, rselt, chot, chott, lhs, contrib, observed,
+    done, grad, resid, turn_in, turn_out, evolved, square,
     zbuf, zsib, zchip, zin, zown, wown, band, sum_out, sum_in,
     local_sem, halo_s, halo_r, sib_s, sib_r, rs_s, rs_r,
     ag_s, ag_r, fw_s, fw_r, sum_s, sum_r,
@@ -80,6 +80,7 @@
 
     def halo_send(ref, which, toward):
         picked = [m for m in range(len(MOVES)) if MOVES[m][0] == toward]
+        picked.sort(key=lambda m: MOVES[m][1] == 0)
 
         def start():
             for m in picked:
@@ -110,7 +111,7 @@
         else:
             wait()
 
-    pieces = local_sem.shape[0] - 1
+    pieces = 4
     chunk = slots // pieces
     jac_copies = [
         pltpu.make_async_copy(
@@ -121,6 +122,14 @@
     kap_copy = pltpu.make_async_copy(
         kh_in, kap.at[MOST:MOST + cells_i, SIDE:SIDE + cells_j, :], local_sem.at[pieces]
     )
+    small_copies = [
+        pltpu.make_async_copy(src, dst, local_sem.at[pieces + 1 + q])
+        for q, (src, dst) in enumerate(
+            ((rows_hbm, rows_in), (innov_hbm, innov), (weight_hbm, weight), (kv_hbm, kv))
+        )
+    ]
+    for copy in small_copies:
+        copy.start()
     kap_copy.start()
     for copy in jac_copies:
         copy.start()
@@ -152,6 +161,8 @@
         return jnp.concatenate([turned[0:half], turned[half:obs]], axis=1)
 
     square[...] = jnp.zeros(square.shape, F32)
+    for copy in small_copies:
+        copy.wait()
     wown[...] = packed(weight[...])
     band[0, core, chip] = wown[...] * packed(innov[...])
 
@@ -167,11 +178,14 @@
         }
         return sent, [remote(mine, mine, fw_s.at[r, 0], fw_r.at[r, 0], a, sibling)]
 
-    def wait_band(r, sent, forwards):
+    def forward_band(r, sent, forwards):
         for d in reversed(order):
             sent[d].wait_recv()
             arrived = band.at[r, core, chip_of(-d)]
             forwards.append(remote(arrived, arrived, fw_s.at[r, d], fw_r.at[r, d], a, sibling))
+        return forwards
+
+    def wait_band(forwards):
         for copy in forwards:
             copy.wait_recv()
 
@@ -206,7 +220,39 @@
     contrib[slots:padded, :] = jnp.zeros((padded - slots, levels), F32)
     observed[slots:padded, :] = jnp.zeros((padded - slots, 128), F32)
 
+    STEPS = levels // 8
+    blocks = columns // 128
+
+    def upended(q, value):
+        turn_in[128 * q:128 * q + 128, :] = jnp.transpose(value)
+        return [turn_in[pl.ds(128 * q + j, 8, stride=STEPS), :] for j in range(STEPS)]
+
+    def restored(q, parts):
+        for j in range(STEPS):
+            turn_out[pl.ds(128 * q + j, 8, stride=STEPS), :] = parts[j]
+        return jnp.transpose(turn_out[128 * q:128 * q + 128, :])
+
+    def keep_parts(ref, q, parts):
+        for j in range(STEPS):
+            ref[128 * q + 8 * j:128 * q + 8 * j + 8, :] = parts[j]
+
+    def kept(ref, q):
+        return [ref[128 * q + 8 * j:128 * q + 8 * j + 8, :] for j in range(STEPS)]
+
+    sublane = lax.broadcasted_iota(jnp.int32, (8, 128), 0)
+    rows_each = 128 // cells_j
+    for q in range(blocks):
+        roots = [
+            jnp.sqrt(part)
+            for part in upended(q, kv[rows_each * q:rows_each * (q + 1)].reshape(128, levels))
+        ]
+        nexts = roots[1:] + [jnp.where(sublane < 7, pltpu.roll(roots[0], 7, 0), 0.0)]
+        keep_parts(vco, q, [root * following for root, following in zip(roots, nexts)])
+
+    forwards = None
     for q, copy in enumerate(jac_copies):
+        if q == pieces - 1:
+            forwards = forward_band(0, *gathering)
         copy.wait()
 
         @pl.loop(q * chunk // 4, (q + 1) * chunk // 4)
@@ -217,43 +263,35 @@
             jparts[0, place, :], jparts[1, place, :] = split(block)
             jturn[0, turned, :], jturn[1, turned, :] = split(jnp.transpose(block))
 
-    level = lax.broadcasted_iota(jnp.int32, (cells_j, levels), 1)
-
-    @pl.loop(0, cells_i)
-    def _(i):
-        root = jnp.sqrt(kv[i])
-        below = jnp.where(level < levels - 1, root * pltpu.roll(root, levels - 1, 1), 0.0)
-        above = jnp.where(level > 0, root * pltpu.roll(root, 1, 1), 0.0)
-        vco[0, i] = 1.0 - below - above
-        vco[1, i] = below
-        vco[2, i] = above
 
     lateral_count = jnp.full((span, levels), counts[0], jnp.int32)
-    vertical_count = jnp.full((cells_j, levels), counts[1], jnp.int32)
-
-    def vertical(rows, values):
+    vertical_count = jnp.full((8, 128), counts[1], jnp.int32)
+
+    def vertical(q, parts):
         for p in range(MOST):
-            news = [
-                vco[0, i] * w + vco[1, i] * pltpu.roll(w, levels - 1, 1) + vco[2, i] * pltpu.roll(w, 1, 1)
-                for i, w in zip(rows, values)
+            faces = kept(vco, q)
+            uppers = parts[1:] + [pltpu.roll(parts[0], 7, 0)]
+            flows = [face * (upper - w) for face, upper, w in zip(faces, uppers, parts)]
+            lowers = [pltpu.roll(flows[-1], 1, 0)] + flows[:-1]
+            news = [w + (flow - lower) for w, flow, lower in zip(parts, flows, lowers)]
+            parts = news if p < LEAST else [
+                jnp.where(vertical_count > p, new, w) for new, w in zip(news, parts)
             ]
-            values = news if p < LEAST else [
-                jnp.where(vertical_count > p, new, w) for new, w in zip(news, values)
-            ]
-        return values
-
-    def lateral(field, target):
-        def rows_of(p, rows):
+        return parts
+
+    def lateral(field, target, meanwhile=lambda: None):
+        def rows_of(p, first, count):
             source = ext.at[field] if p == 0 else tmp.at[p - 1]
+            ws = [source[first + q] for q in range(-1, count + 1)]
+            flows = [lco[0, first + q - 1] * (ws[q + 1] - ws[q]) for q in range(count + 1)]
             news = []
-            for i in rows:
-                w = source[i]
-                new = (
-                    lco[0, i] * w + lco[1, i] * source[i - 1] + lco[2, i] * source[i + 1]
-                    + lco[3, i] * pltpu.roll(w, 1, 0) + lco[4, i] * pltpu.roll(w, span - 1, 0)
-                )
+            for q in range(count):
+                w = ws[q + 1]
+                east = lco[1, first + q] * (pltpu.roll(w, span - 1, 0) - w)
+                new = w + (flows[q + 1] - flows[q]) + (east - pltpu.roll(east, 1, 0))
                 news.append(new if p < LEAST else jnp.where(lateral_count > p, new, w))
-            for i, new in zip(rows, news):
+            for q, new in enumerate(news):
+                i = first + q
                 if p < MOST - 1:
                     tmp[p, i] = new
                 else:
@@ -265,10 +303,11 @@
         halo_wait(ext.at[field], field + 1, 0)
         for p in range(MOST):
             first = MOST + p + 1
-
-            @pl.loop(0, (cells_i - 2 * p - 2) // 2)
-            def _(g, p=p, first=first):
-                rows_of(p, [first + 2 * g, first + 2 * g + 1])
+            count = cells_i // 2 - p - 1
+
+            @pl.loop(0, 2)
+            def _(g, p=p, first=first, count=count):
+                rows_of(p, first + count * g, count)
 
         halo_wait(ext.at[field], field + 1, -1)
         halo_wait(ext.at[field], field + 1, 1)
@@ -276,9 +315,11 @@
             top = p + 1
             low = MOST + cells_i - p - 1
 
-            @pl.loop(0, MOST // 2)
+            @pl.loop(0, 2)
             def _(g, p=p, top=top, low=low):
-                rows_of(p, [top + 2 * g, top + 2 * g + 1, low + 2 * g, low + 2 * g + 1])
+                rows_of(p, top + (low - top) * g, MOST)
+
+        return meanwhile()
 
     def send_sum(i, tile, along_lat):
         sum_out[i] = tile
@@ -397,7 +438,7 @@
             jnp.where(sub8 == 1, jnp.sum(second, axis=0, keepdims=True), 0.0),
         )
 
-    wait_band(0, *gathering)
+    wait_band(forwards)
     adjoint(0, 0)
     halo(ext.at[0], 1)
 
@@ -409,36 +450,27 @@
         for u in range(2):
             tmp[0, 2 * g + u] = jnp.sqrt(kap[2 * g + u])
 
-    @pl.loop(0, total_rows // 2 - 1)
+    @pl.loop(0, total_rows // 2)
     def _(g):
         for u in range(2):
-            i = 2 * g + 1 + u
+            i = 2 * g + u
             root = tmp[0, i]
-            up = root * tmp[0, i - 1]
-            down = root * tmp[0, i + 1]
-            west = root * pltpu.roll(root, 1, 0)
-            east = root * pltpu.roll(root, span - 1, 0)
-            lco[0, i] = 1.0 - (up + down + west + east)
-            lco[1, i] = up
-            lco[2, i] = down
-            lco[3, i] = west
-            lco[4, i] = east
-
-    def row(ref, i):
-        return ref[i * cells_j:(i + 1) * cells_j, :]
-
-    def middle(field, i, value):
-        ext[field, MOST + i, SIDE:SIDE + cells_j, :] = value
-
-    GROUP = 8
-    groups = [list(range(q, q + GROUP)) for q in range(0, cells_i, GROUP)]
+            lco[0, i] = root * tmp[0, jnp.minimum(i + 1, total_rows - 1)]
+            lco[1, i] = root * pltpu.roll(root, span - 1, 0)
+
+    def block_of(ref, q):
+        return ref[128 * q:128 * q + 128, :]
+
+    def middle(field, q, value):
+        rows = slice(MOST + rows_each * q, MOST + rows_each * (q + 1))
+        ext[field, rows, SIDE:SIDE + cells_j, :] = value.reshape(rows_each, cells_j, levels)
 
     def spread_and_send(field, work):
         accs = None
-        for q, rows in enumerate(groups):
-            parts = work(rows)
+        for q in range(blocks):
+            parts = work(q)
             accs = parts if accs is None else [x + y for x, y in zip(accs, parts)]
-            if q == 0:
+            if q == blocks // 2 - 1:
                 halo_send(ext.at[field], field + 1, -1)
         halo_send(ext.at[field], field + 1, 1)
         halo_send(ext.at[field], field + 1, 0)
@@ -446,19 +478,15 @@
 
     lateral(0, done)
 
-    def gradient_rows(rows):
-        ws = vertical(rows, [row(done, i) for i in rows])
-        total = sum(fold(w * w) for w in ws)
-        nexts = vertical(rows, ws)
-        for i, w, following in zip(rows, ws, nexts):
-            grad[i] = w
-            middle(1, i, following)
-        return [total]
-
-    (total,) = spread_and_send(1, gradient_rows)
+    def gradient_block(q):
+        ws = vertical(q, upended(q, block_of(done, q)))
+        keep_parts(grad, q, ws)
+        middle(1, q, restored(q, vertical(q, ws)))
+        return [sum(w * w for w in ws)]
+
+    (total,) = spread_and_send(1, gradient_block)
     norm_lat = send_sum(0, total, True)
-    lateral(1, evolved.at[0])
-    norm_lon = send_sum(1, take_sum(0, norm_lat), False)
+    norm_lon = lateral(1, evolved.at[0], lambda: send_sum(1, take_sum(0, norm_lat), False))
 
     piece = observe(0, 0)
     zown[...] = piece
@@ -467,30 +495,25 @@
     gathering = send_band(1)
     curve_lat = send_sum(2, fold(weighted * piece), True)
     norm = whole(take_sum(1, norm_lon))
-    wait_band(1, *gathering)
+    wait_band(forward_band(1, *gathering))
     adjoint(1, 2)
     halo(ext.at[2], 3)
     curve_lon = send_sum(3, take_sum(2, curve_lat), False)
     lateral(2, done)
     alpha_first = norm / (norm + whole(take_sum(3, curve_lon)))
-    alpha_wide = jnp.broadcast_to(alpha_first, (cells_j, levels))
-
-    def residual_rows(rows):
-        ws = vertical(rows, [row(done, i) for i in rows])
-        gs = [grad[i] for i in rows]
+    alpha_wide = jnp.broadcast_to(alpha_first, (8, 128))
+
+    def residual_block(q):
+        ws = vertical(q, upended(q, block_of(done, q)))
+        gs = kept(grad, q)
         news = [g - alpha_wide * (g + w) for g, w in zip(gs, ws)]
-        squares = sum(fold(new * new) for new in news)
-        crosses = sum(fold(new * g) for new, g in zip(news, gs))
-        nexts = vertical(rows, news)
-        for i, new, following in zip(rows, news, nexts):
-            resid[i] = new
-            middle(3, i, following)
-        return [squares, crosses]
-
-    squares, crosses = spread_and_send(3, residual_rows)
+        keep_parts(resid, q, news)
+        middle(3, q, restored(q, vertical(q, news)))
+        return [sum(new * new for new in news), sum(new * g for new, g in zip(news, gs))]
+
+    squares, crosses = spread_and_send(3, residual_block)
     norm_lat = send_sum(4, two_rows(squares, crosses), True)
-    lateral(3, evolved.at[1])
-    norm_lon = send_sum(5, take_sum(4, norm_lat), False)
+    norm_lon = lateral(3, evolved.at[1], lambda: send_sum(5, take_sum(4, norm_lat), False))
 
     piece = observe(1, 1)
     tile = take_sum(5, norm_lon)
@@ -503,21 +526,27 @@
     band[2, core, chip] = weighted
     gathering = send_band(2)
     curve_lat = send_sum(6, fold(weighted * piece), True)
-    wait_band(2, *gathering)
+    wait_band(forward_band(2, *gathering))
     adjoint(2, 4)
     halo(ext.at[4], 5)
     curve_lon = send_sum(7, take_sum(6, curve_lat), False)
     lateral(4, done)
     alpha_second = norm_next / (self_product + whole(take_sum(7, curve_lon)))
-    second_wide = jnp.broadcast_to(alpha_second, (cells_j, levels))
-    beta_wide = jnp.broadcast_to(beta, (cells_j, levels))
-    for rows in groups:
-        ws = vertical(rows, [row(done, i) for i in rows])
-        for i, w in zip(rows, ws):
-            r = resid[i]
-            residual_out[i] = r - second_wide * (r + beta_wide * grad[i] + w)
-            first, second = row(evolved.at[0], i), row(evolved.at[1], i)
-            increment[i] = alpha_wide * first + second_wide * (second + beta_wide * first)
+    second_wide = jnp.broadcast_to(alpha_second, (8, 128))
+    beta_wide = jnp.broadcast_to(beta, (8, 128))
+    for q in range(blocks):
+        ws = vertical(q, upended(q, block_of(done, q)))
+        lasts = [
+            r - second_wide * (r + beta_wide * g + w)
+            for r, g, w in zip(kept(resid, q), kept(grad, q), ws)
+        ]
+        rows = slice(rows_each * q, rows_each * (q + 1))
+        residual_out[rows] = restored(q, lasts).reshape(rows_each, cells_j, levels)
+    for i in range(cells_i):
+        first = evolved[0, i * cells_j:(i + 1) * cells_j, :]
+        second = evolved[1, i * cells_j:(i + 1) * cells_j, :]
+        scale = alpha_first + alpha_second * beta
+        increment[i] = scale * first + alpha_second * second
 
     for copy in started:
         copy.wait_send()
@@ -525,6 +554,17 @@
         ref = kap if which == 0 else ext.at[which - 1]
         for toward in (-1, 0, 1):
             halo_wait(ref, which, toward, sent=True)
+
+
+def hand_over(first, second, first_out, second_out, sems):
+    copies = [
+        pltpu.make_async_copy(first, first_out, sems.at[0]),
+        pltpu.make_async_copy(second, second_out, sems.at[1]),
+    ]
+    for copy in copies:
+        copy.start()
+    for copy in copies:
+        copy.wait()
 
 
 def local(n_lat, n_lon, innovation, obs_weight, jacobian, block_list, pass_counts, kappa_h, kappa_v):
@@ -544,20 +584,24 @@
     in_vmem = pl.BlockSpec(memory_space=pltpu.VMEM)
     in_smem = pl.BlockSpec(memory_space=pltpu.SMEM)
     in_any = pl.BlockSpec(memory_space=pl.ANY)
-    return pl.pallas_call(
+    results = pl.pallas_call(
         functools.partial(kernel, shape),
         out_shape=(field, field),
-        in_specs=[in_smem, in_vmem, in_vmem, in_vmem, in_any, in_any, in_vmem],
+        in_specs=[in_smem] + [in_any] * 6,
         out_specs=(in_vmem, in_vmem),
         scratch_shapes=[
+            vmem(block_list.shape, jnp.int32),
+            vmem(innovation.shape, F32),
+            vmem(obs_weight.shape, F32),
+            vmem((cells_i, cells_j, levels), F32),
             vmem((slots, obs, levels), F32),
             vmem((2, slots * obs, levels), BF16),
             vmem((2, slots // 4 * levels, 4 * obs), BF16),
             vmem((total_rows, span, levels), F32),
             vmem((5, total_rows, span, levels), F32),
             vmem((MOST - 1, total_rows, span, levels), F32),
-            vmem((5, total_rows, span, levels), F32),
-            vmem((3, cells_i, cells_j, levels), F32),
+            vmem((2, total_rows, span, levels), F32),
+            vmem((columns, levels), F32),
             vmem((8, padded), jnp.int32),
             vmem((2, padded, half * n_lon), BF16),
             vmem((2, half * n_lon, padded), BF16),
@@ -567,8 +611,10 @@
             vmem((padded, levels), F32),
             vmem((padded, 128), F32),
             vmem((columns, levels), F32),
-            vmem((cells_i, cells_j, levels), F32),
-            vmem((cells_i, cells_j, levels), F32),
+            vmem((columns, levels), F32),
+            vmem((columns, levels), F32),
+            vmem((columns, levels), F32),
+            vmem((columns, levels), F32),
             vmem((2, columns, levels), F32),
             vmem((128, 128), F32),
             vmem((2, 2, chips, half, 128), F32),
@@ -580,7 +626,7 @@
             vmem((3, 2, chips, half, 128), F32),
             vmem((8, 8, 128), F32),
             vmem((8, peers, 8, 128), F32),
-            dma((5,)),
+            dma((9,)),
             dma((6, 8)), dma((6, 8)),
             dma((2,)), dma((2,)),
             dma((2, chips - 1)), dma((2, chips - 1)),
@@ -592,6 +638,13 @@
             collective_id=0, has_side_effects=True, vmem_limit_bytes=60 * 1024 * 1024
         ),
     )(pass_counts, block_list, innovation, obs_weight, jacobian, kappa_h, kappa_v)
+    return pl.pallas_call(
+        hand_over,
+        out_shape=(field, field),
+        in_specs=[in_vmem, in_vmem],
+        out_specs=(in_any, in_any),
+        scratch_shapes=[dma((2,))],
+    )(*results)
 
 
 def solution(mesh):

time: 102 us -> 95.6 us (0.937)
  local copies, waits for them, and re-layouts: 3.34 us -> 0 us
  Pallas kernels: 96.9 us -> 93.8 us
    pallas_call x1, Pallas kernels: 96.9 us -> 92 us  [local(): pl.pallas_call(functools.partial(kernel, shape), out_shape=(field, field)...]
    unnamed x2 -> x0, local copies, waits for them, and re-layouts: 3.34 us -> none
    pallas_call x0 -> x1, Pallas kernels: none -> 1.83 us  [local(): pl.pallas_call(hand_over, out_shape=(field, field), in_specs=[in_vmem, in...]
where the time goes in v3:
time: 95.6 us; the launch traced here: 94.5 us
  Pallas kernels  93.8 us (98%)
    pallas_call x1, Pallas kernels, local(): pl.pallas_call(functools.partial(kernel, shape), out_shape=(field, field)...  92 us

profile of v3, /device:TPU:9, one launch (start us, length us, event | category | flops | bytes accessed | tf_op | source)
XLA Modules:
  0.0 94.5 jit_solution(1791193333742225070)
XLA Ops:
  0.6 92.0 %shard_map.86 = (f32[16,32,128]{2,1,0:T(8,128)}, f32[16,32,128]{2,1,0:T(8,128)}) custom-call(s32[2]{0:T(128)} %counts.1, s32[2,192]{1,0:T(2,128)} %rows_hbm.1, f32[64,64]{1,0:T(8,128)} %innov_hbm.1, f32[64,64]{1,0:T(8,128)} %weight_hbm.1, f32[192,64,128]{2,1,0:T(8,128)} %jac_in.1, f32[16,32,128]{2,1,0:T(8,128)} %kh_in.1, f32[16,32,128]{2,1,0:T(8,128)} %kv_hbm.1), custom_call_target="tpu_custom_call" | custom-call | tf_op jit(solution)/shard_map/pallas_call | solution.py:587
  92.6 1.8 %shard_map.87 = (f32[16,32,128]{2,1,0:T(8,128)}, f32[16,32,128]{2,1,0:T(8,128)}) custom-call(f32[16,32,128]{2,1,0:T(8,128)} %get-tuple-element.4.first, f32[16,32,128]{2,1,0:T(8,128)} %get-tuple-element.5.second), custom_call_target="tpu_custom_call" | custom-call | tf_op jit(solution)/shard_map/pallas_call | solution.py:641

commit v4 on v3

--- a/solution.py
+++ b/solution.py
@@ -31,7 +31,7 @@
     shape, counts, rows_hbm, innov_hbm, weight_hbm, jac_in, kh_in, kv_hbm,
     increment, residual_out,
     rows_in, innov, weight, kv, jac, jparts, jturn, kap, ext, tmp, lco, vco, lst, rsel, rselt, chot, chott, lhs, contrib, observed,
-    done, grad, resid, turn_in, turn_out, evolved, square,
+    done, grad, resid, image, turn_in, turn_out, evolved, square,
     zbuf, zsib, zchip, zin, zown, wown, band, sum_out, sum_in,
     local_sem, halo_s, halo_r, sib_s, sib_r, rs_s, rs_r,
     ag_s, ag_r, fw_s, fw_r, sum_s, sum_r,
@@ -279,7 +279,7 @@
             ]
         return parts
 
-    def lateral(field, target, meanwhile=lambda: None):
+    def lateral(field, target):
         def rows_of(p, first, count):
             source = ext.at[field] if p == 0 else tmp.at[p - 1]
             ws = [source[first + q] for q in range(-1, count + 1)]
@@ -319,7 +319,6 @@
             def _(g, p=p, top=top, low=low):
                 rows_of(p, top + (low - top) * g, MOST)
 
-        return meanwhile()
 
     def send_sum(i, tile, along_lat):
         sum_out[i] = tile
@@ -427,16 +426,15 @@
     def fold(value):
         return jnp.sum(value.reshape(value.shape[0] // 8, 8, levels), axis=0)
 
-    def whole(value):
-        return jnp.sum(jnp.sum(value, axis=0, keepdims=True), axis=1, keepdims=True)
-
-    def two_rows(first, second):
-        sub8 = lax.broadcasted_iota(jnp.int32, (8, levels), 0)
-        return jnp.where(
-            sub8 == 0,
-            jnp.sum(first, axis=0, keepdims=True),
-            jnp.where(sub8 == 1, jnp.sum(second, axis=0, keepdims=True), 0.0),
-        )
+    def stacked(parts):
+        rows = lax.broadcasted_iota(jnp.int32, (8, levels), 0)
+        tile = jnp.zeros((8, levels), F32)
+        for i, part in enumerate(parts):
+            tile = jnp.where(rows == i, jnp.sum(part, axis=0, keepdims=True), tile)
+        return tile
+
+    def entry(tile, i):
+        return jnp.sum(tile[i:i + 1, :], axis=1, keepdims=True)
 
     wait_band(forwards)
     adjoint(0, 0)
@@ -485,22 +483,22 @@
         return [sum(w * w for w in ws)]
 
     (total,) = spread_and_send(1, gradient_block)
-    norm_lat = send_sum(0, total, True)
-    norm_lon = lateral(1, evolved.at[0], lambda: send_sum(1, take_sum(0, norm_lat), False))
+    lateral(1, evolved.at[0])
 
     piece = observe(0, 0)
     zown[...] = piece
     weighted = wown[...] * piece
     band[1, core, chip] = weighted
     gathering = send_band(1)
-    curve_lat = send_sum(2, fold(weighted * piece), True)
-    norm = whole(take_sum(1, norm_lon))
+    sums_lat = send_sum(0, stacked([total, fold(weighted * piece)]), True)
     wait_band(forward_band(1, *gathering))
     adjoint(1, 2)
     halo(ext.at[2], 3)
-    curve_lon = send_sum(3, take_sum(2, curve_lat), False)
+    sums_lon = send_sum(1, take_sum(0, sums_lat), False)
     lateral(2, done)
-    alpha_first = norm / (norm + whole(take_sum(3, curve_lon)))
+    tile = take_sum(1, sums_lon)
+    norm, curve = entry(tile, 0), entry(tile, 1)
+    alpha_first = norm / (norm + curve)
     alpha_wide = jnp.broadcast_to(alpha_first, (8, 128))
 
     def residual_block(q):
@@ -508,37 +506,38 @@
         gs = kept(grad, q)
         news = [g - alpha_wide * (g + w) for g, w in zip(gs, ws)]
         keep_parts(resid, q, news)
+        keep_parts(image, q, ws)
         middle(3, q, restored(q, vertical(q, news)))
         return [sum(new * new for new in news), sum(new * g for new, g in zip(news, gs))]
 
     squares, crosses = spread_and_send(3, residual_block)
-    norm_lat = send_sum(4, two_rows(squares, crosses), True)
-    norm_lon = lateral(3, evolved.at[1], lambda: send_sum(5, take_sum(4, norm_lat), False))
+    lateral(3, evolved.at[1])
 
     piece = observe(1, 1)
-    tile = take_sum(5, norm_lon)
-    norm_next = jnp.sum(tile[0:1, :], axis=1, keepdims=True)
-    cross = jnp.sum(tile[1:2, :], axis=1, keepdims=True)
-    beta = norm_next / norm
-    self_product = norm_next + 2.0 * beta * cross + beta * beta * norm
-    piece = piece + beta * zown[...]
     weighted = wown[...] * piece
     band[2, core, chip] = weighted
     gathering = send_band(2)
-    curve_lat = send_sum(6, fold(weighted * piece), True)
+    sums_lat = send_sum(
+        2, stacked([squares, crosses, fold(weighted * piece), fold(weighted * zown[...])]), True
+    )
     wait_band(forward_band(2, *gathering))
     adjoint(2, 4)
     halo(ext.at[4], 5)
-    curve_lon = send_sum(7, take_sum(6, curve_lat), False)
+    sums_lon = send_sum(3, take_sum(2, sums_lat), False)
     lateral(4, done)
-    alpha_second = norm_next / (self_product + whole(take_sum(7, curve_lon)))
+    tile = take_sum(3, sums_lon)
+    norm_next, cross = entry(tile, 0), entry(tile, 1)
+    beta = norm_next / norm
+    self_product = norm_next + 2.0 * beta * cross + beta * beta * norm
+    curve_next = entry(tile, 2) + 2.0 * beta * entry(tile, 3) + beta * beta * curve
+    alpha_second = norm_next / (self_product + curve_next)
     second_wide = jnp.broadcast_to(alpha_second, (8, 128))
     beta_wide = jnp.broadcast_to(beta, (8, 128))
     for q in range(blocks):
         ws = vertical(q, upended(q, block_of(done, q)))
         lasts = [
-            r - second_wide * (r + beta_wide * g + w)
-            for r, g, w in zip(kept(resid, q), kept(grad, q), ws)
+            r - second_wide * (r + w + beta_wide * (g + v))
+            for r, g, v, w in zip(kept(resid, q), kept(grad, q), kept(image, q), ws)
         ]
         rows = slice(rows_each * q, rows_each * (q + 1))
         residual_out[rows] = restored(q, lasts).reshape(rows_each, cells_j, levels)
@@ -615,6 +614,7 @@
             vmem((columns, levels), F32),
             vmem((columns, levels), F32),
             vmem((columns, levels), F32),
+            vmem((columns, levels), F32),
             vmem((2, columns, levels), F32),
             vmem((128, 128), F32),
             vmem((2, 2, chips, half, 128), F32),
@@ -624,15 +624,15 @@
             vmem((half, 128), F32),
             vmem((half, 128), F32),
             vmem((3, 2, chips, half, 128), F32),
-            vmem((8, 8, 128), F32),
-            vmem((8, peers, 8, 128), F32),
+            vmem((4, 8, 128), F32),
+            vmem((4, peers, 8, 128), F32),
             dma((9,)),
             dma((6, 8)), dma((6, 8)),
             dma((2,)), dma((2,)),
             dma((2, chips - 1)), dma((2, chips - 1)),
             dma((3, chips)), dma((3, chips)),
             dma((3, chips)), dma((3, chips)),
-            dma((8, peers)), dma((8, peers)),
+            dma((4, peers)), dma((4, peers)),
         ],
         compiler_params=pltpu.CompilerParams(
             collective_id=0, has_side_effects=True, vmem_limit_bytes=60 * 1024 * 1024

time: 95.6 us -> 92.8 us (0.971); the launches traced: 94.5 us -> 92.6 us
  Pallas kernels: 93.8 us -> 92 us
    pallas_call x1, Pallas kernels: 92 us -> 90.2 us  [local(): pl.pallas_call(functools.partial(kernel, shape), out_shape=(field, field)...]
where the time goes in v4:
time: 92.8 us; the launch traced here: 92.6 us
  Pallas kernels  92 us (99%)
    pallas_call x1, Pallas kernels, local(): pl.pallas_call(functools.partial(kernel, shape), out_shape=(field, field)...  90.2 us

profile of v4, /device:TPU:9, one launch (start us, length us, event | category | flops | bytes accessed | tf_op | source)
XLA Modules:
  0.0 92.6 jit_solution(6574035234742362307)
XLA Ops:
  0.6 90.2 %shard_map.86 = (f32[16,32,128]{2,1,0:T(8,128)}, f32[16,32,128]{2,1,0:T(8,128)}) custom-call(s32[2]{0:T(128)} %counts.1, s32[2,192]{1,0:T(2,128)} %rows_hbm.1, f32[64,64]{1,0:T(8,128)} %innov_hbm.1, f32[64,64]{1,0:T(8,128)} %weight_hbm.1, f32[192,64,128]{2,1,0:T(8,128)} %jac_in.1, f32[16,32,128]{2,1,0:T(8,128)} %kh_in.1, f32[16,32,128]{2,1,0:T(8,128)} %kv_hbm.1), custom_call_target="tpu_custom_call" | custom-call | tf_op jit(solution)/shard_map/pallas_call | solution.py:586
  90.8 1.8 %shard_map.87 = (f32[16,32,128]{2,1,0:T(8,128)}, f32[16,32,128]{2,1,0:T(8,128)}) custom-call(f32[16,32,128]{2,1,0:T(8,128)} %get-tuple-element.4.first, f32[16,32,128]{2,1,0:T(8,128)} %get-tuple-element.5.second), custom_call_target="tpu_custom_call" | custom-call | tf_op jit(solution)/shard_map/pallas_call | solution.py:641

commit v5 on v4

--- a/solution.py
+++ b/solution.py
@@ -406,16 +406,22 @@
             for k in range(2):
                 first = half * (2 * c + k)
                 zbuf[r, k, c] = partial[first:first + half, :]
-        remote(zbuf.at[r, 1 - core], zsib.at[r], sib_s.at[r], sib_r.at[r], a, sibling).wait_recv()
-        for c in range(chips):
+        halves = {}
+        for d in order + [0]:
+            c = chip_of(d)
+            halves[d] = remote(
+                zbuf.at[r, 1 - core, c], zsib.at[r, c], sib_s.at[r, d], sib_r.at[r, d], a, sibling
+            )
+        copies = []
+        for d in order + [0]:
+            c = chip_of(d)
+            halves[d].wait_recv()
             zchip[r, c] = zbuf[r, core, c] + zsib[r, c]
-        copies = [
-            remote(
-                zchip.at[r, chip_of(d)], zin.at[r, d - 1], rs_s.at[r, d - 1], rs_r.at[r, d - 1],
-                a, chip_of(d) * 2 + core,
-            )
-            for d in order
-        ]
+            if d:
+                copies.append(remote(
+                    zchip.at[r, c], zin.at[r, d - 1], rs_s.at[r, d - 1], rs_r.at[r, d - 1],
+                    a, c * 2 + core,
+                ))
         total = zchip[r, chip]
         for copy in copies:
             copy.wait_recv()
@@ -628,7 +634,7 @@
             vmem((4, peers, 8, 128), F32),
             dma((9,)),
             dma((6, 8)), dma((6, 8)),
-            dma((2,)), dma((2,)),
+            dma((2, chips)), dma((2, chips)),
             dma((2, chips - 1)), dma((2, chips - 1)),
             dma((3, chips)), dma((3, chips)),
             dma((3, chips)), dma((3, chips)),

time: 92.8 us -> 92.5 us (level)
  no operation moved by 1% of the time
where the time goes in v5:
time: 92.5 us; the launch traced here: 92.3 us
  Pallas kernels  91.7 us (99%)
    pallas_call x1, Pallas kernels, local(): pl.pallas_call(functools.partial(kernel, shape), out_shape=(field, field)...  89.8 us

profile of v5, /device:TPU:9, one launch (start us, length us, event | category | flops | bytes accessed | tf_op | source)
XLA Modules:
  0.0 92.3 jit_solution(8414671041353424248)
XLA Ops:
  0.6 89.8 %shard_map.86 = (f32[16,32,128]{2,1,0:T(8,128)}, f32[16,32,128]{2,1,0:T(8,128)}) custom-call(s32[2]{0:T(128)} %counts.1, s32[2,192]{1,0:T(2,128)} %rows_hbm.1, f32[64,64]{1,0:T(8,128)} %innov_hbm.1, f32[64,64]{1,0:T(8,128)} %weight_hbm.1, f32[192,64,128]{2,1,0:T(8,128)} %jac_in.1, f32[16,32,128]{2,1,0:T(8,128)} %kh_in.1, f32[16,32,128]{2,1,0:T(8,128)} %kv_hbm.1), custom_call_target="tpu_custom_call" | custom-call | tf_op jit(solution)/shard_map/pallas_call | solution.py:592
  90.5 1.8 %shard_map.87 = (f32[16,32,128]{2,1,0:T(8,128)}, f32[16,32,128]{2,1,0:T(8,128)}) custom-call(f32[16,32,128]{2,1,0:T(8,128)} %get-tuple-element.4.first, f32[16,32,128]{2,1,0:T(8,128)} %get-tuple-element.5.second), custom_call_target="tpu_custom_call" | custom-call | tf_op jit(solution)/shard_map/pallas_call | solution.py:647

commit v6 on v5

--- a/solution.py
+++ b/solution.py
@@ -111,6 +111,16 @@
         else:
             wait()
 
+    far_first = sorted(range(1, n_lon), key=lambda d: -min(d, n_lon - d))
+    partners = [(a, lon_of(d)) for d in far_first]
+    partners += [(lat_of(i), lon_of(j)) for i, j in MOVES if i and j]
+    partners += [(lat_of(d), b) for d in range(1, n_lat)]
+    barrier = pltpu.get_barrier_semaphore()
+    for to_lat, to_lon in partners:
+        pl.semaphore_signal(
+            barrier, inc=1, device_id=(to_lat, to_lon), device_id_type=pl.DeviceIdType.MESH
+        )
+
     pieces = 4
     chunk = slots // pieces
     jac_copies = [
@@ -133,15 +143,6 @@
     kap_copy.start()
     for copy in jac_copies:
         copy.start()
-
-    partners = [(lat_of(i), lon_of(j)) for i, j in MOVES if i and j]
-    partners += [(lat_of(d), b) for d in range(1, n_lat)]
-    partners += [(a, lon_of(d)) for d in range(1, n_lon)]
-    barrier = pltpu.get_barrier_semaphore()
-    for to_lat, to_lon in partners:
-        pl.semaphore_signal(
-            barrier, inc=1, device_id=(to_lat, to_lon), device_id_type=pl.DeviceIdType.MESH
-        )
 
     @pl.when(a == 0)
     def _():

time: 92.5 us -> 92.3 us (level)
  no operation moved by 1% of the time
where the time goes in v6:
time: 92.3 us; the launch traced here: 92.1 us
  Pallas kernels  91.4 us (99%)
    pallas_call x1, Pallas kernels, local(): pl.pallas_call(functools.partial(kernel, shape), out_shape=(field, field)...  89.6 us

profile of v6, /device:TPU:9, one launch (start us, length us, event | category | flops | bytes accessed | tf_op | source)
XLA Modules:
  0.0 92.1 jit_solution(2499022491049722810)
XLA Ops:
  0.6 89.6 %shard_map.86 = (f32[16,32,128]{2,1,0:T(8,128)}, f32[16,32,128]{2,1,0:T(8,128)}) custom-call(s32[2]{0:T(128)} %counts.1, s32[2,192]{1,0:T(2,128)} %rows_hbm.1, f32[64,64]{1,0:T(8,128)} %innov_hbm.1, f32[64,64]{1,0:T(8,128)} %weight_hbm.1, f32[192,64,128]{2,1,0:T(8,128)} %jac_in.1, f32[16,32,128]{2,1,0:T(8,128)} %kh_in.1, f32[16,32,128]{2,1,0:T(8,128)} %kv_hbm.1), custom_call_target="tpu_custom_call" | custom-call | tf_op jit(solution)/shard_map/pallas_call | solution.py:593
  90.2 1.8 %shard_map.87 = (f32[16,32,128]{2,1,0:T(8,128)}, f32[16,32,128]{2,1,0:T(8,128)}) custom-call(f32[16,32,128]{2,1,0:T(8,128)} %get-tuple-element.4.first, f32[16,32,128]{2,1,0:T(8,128)} %get-tuple-element.5.second), custom_call_target="tpu_custom_call" | custom-call | tf_op jit(solution)/shard_map/pallas_call | solution.py:648
